TPU v7x, 256 devices: a whole 4x4x8 slice. The times are simulated.
256 devices in a mesh: branch: 2 (over core), seq: 8 (over y, x_hi), rep: 16 (over z, x_lo).
Axes of the slice: x: 4 (x_hi: 2, x_lo: 2; x = x_hi * 2 + x_lo), y: 4, z: 8, core: 2. Of those that a mesh axis runs over, the one named last changes fastest.
Arguments:
- queries: bfloat16 [2, 16384, 2048], P('branch', ('rep', 'seq')), parts along dimension 1, may hold values from -64 to 64
- key_vecs: bfloat16 [2, 16384, 2048], P('branch', ('rep', 'seq')), parts along dimension 1, may hold values from -8 to 8
- value_vecs: bfloat16 [2, 16384, 2048], P('branch', ('rep', 'seq')), parts along dimension 1, may hold values from -6 to 6
- hidden_in: bfloat16 [2, 16384, 2048], P('branch', ('rep', 'seq')), parts along dimension 1, may hold values from -4 to 4
- out_proj: bfloat16 [2, 2048, 2048], P('branch', 'seq'), may hold values from -0.125 to 0.125
- couple_proj: bfloat16 [2, 2048, 2048], P('branch', 'seq'), may hold values from -0.125 to 0.125
- grad_mixed: bfloat16 [2, 16384, 2048], P('branch', ('rep', 'seq')), parts along dimension 1, may hold values from -6 to 6
Outputs:
- mixed_out: bfloat16 [2, 16384, 2048], P('branch', ('rep', 'seq')), parts along dimension 1
- grad_hidden: bfloat16 [2, 16384, 2048], P('branch', ('rep', 'seq')), parts along dimension 1
- grad_queries: bfloat16 [2, 16384, 2048], P('branch', ('rep', 'seq')), parts along dimension 1
- grad_keys: bfloat16 [2, 16384, 2048], P('branch', ('rep', 'seq')), parts along dimension 1
- grad_values: bfloat16 [2, 16384, 2048], P('branch', ('rep', 'seq')), parts along dimension 1
- grad_couple: float32 [2, 2048, 32768], P('branch', 'seq', 'rep'), parts along dimension 2
There are 16 independent parts, one for each index of `rep`. A program takes and returns all parts, laid end to end along the dimension named above; an argument that names none is the same for every part. Nothing has to cross between parts.
All inputs are finite; a program needn't handle non-finite values.
Results may differ from a plain program's by a relative error of at most 0.015.
Values may be sent and summed in bfloat16 or wider, within the bound.
No kernel may reach another device: no remote copies, remote signals or barrier semaphores. Data moves between devices by JAX's collectives and lax.ppermute only.
A program may use at most 128 MiB of HBM per device.

v0:
```python
import math

import jax
import jax.numpy as jnp
from jax import lax
from jax.experimental import pallas as pl
from jax.experimental.pallas import tpu as pltpu
from jax.sharding import PartitionSpec as P


HEAD = 128
TOK = 128
CHUNK = 256
WIDE = 2 * CHUNK
FACTOR = 1.0 / math.sqrt(HEAD)
BF16 = jnp.bfloat16
F32 = jnp.float32
VMEM_LIMIT = 56 * 1024 * 1024


def seq_shift(value, mask):
    size = lax.axis_size("seq")
    return lax.ppermute(value, "seq", [(i, i ^ mask) for i in range(size)])


def branch_swap(value):
    return lax.ppermute(value, "branch", [(0, 1), (1, 0)])


def rep_shift(value, mask):
    seqs, reps = lax.axis_size("seq"), lax.axis_size("rep")
    pairs = [
        (s * reps + r, (s ^ mask) * reps + (r ^ 1)) for s in range(seqs) for r in range(reps)
    ]
    return lax.ppermute(value, ("seq", "rep"), pairs)


def half_rows(weight, odd_rep):
    return lax.dynamic_slice(weight, (HEAD * (1 - odd_rep), 0), (HEAD, weight.shape[1]))


def dot(left, right, left_dim, right_dim):
    return lax.dot_general(
        left, right, (((left_dim,), (right_dim,)), ((), ())), preferred_element_type=F32
    )


def full(shape):
    return pl.BlockSpec(shape, lambda *_: (0,) * len(shape))


def call(body, in_specs, out_blocks, out_shapes, place, args, scratch=()):
    specs = list(in_specs) + [full(arg.shape) for arg in args[len(in_specs) :]]
    return pl.pallas_call(
        body,
        out_shape=out_shapes,
        grid_spec=pltpu.PrefetchScalarGridSpec(
            num_scalar_prefetch=1,
            grid=(1,),
            in_specs=specs,
            out_specs=[full(block) for block in out_blocks],
            scratch_shapes=list(scratch),
        ),
        compiler_params=pltpu.CompilerParams(vmem_limit_bytes=VMEM_LIMIT),
    )(place, *args)


def sds(shape, dtype=BF16):
    return jax.ShapeDtypeStruct(shape, dtype)


def chunk(place, rel):
    return pl.ds(pl.multiple_of((place[0] ^ rel) * CHUNK, CHUNK), CHUNK)


def held_rows(place, mine, other, cols):
    first, second = mine[:, cols], other[:, cols]
    odd = place[1] == 1
    return jnp.concatenate(
        [jnp.where(odd, second, first), jnp.where(odd, first, second)], axis=0
    )


def stacked(refs):
    return jnp.concatenate([ref[...] for ref in refs], axis=0)


def block_rows(r):
    return slice(r * TOK, (r + 1) * TOK)


def relative_columns(place, arrays):
    count = len(arrays)

    def body(place_ref, *refs):
        ins, outs = refs[:count], refs[count:]
        for a in range(count):
            for rel in range(8):
                half = rel & 1
                outs[rel >> 1][a, :, half * CHUNK : (half + 1) * CHUNK] = ins[a][
                    :, chunk(place_ref, rel)
                ]

    shape = (count, TOK, WIDE)
    return call(body, [], [shape] * 4, [sds(shape)] * 4, place, arrays)


def back_couple_product(place, grads, couple):
    def body(place_ref, g0, g1, g2, g3, own, mine, other, out, picked):
        rows = stacked((g0, g1, g2, g3))
        held = held_rows(place_ref, mine, other, slice(None))
        out[:, :CHUNK] = dot(rows, own[...], 1, 1).astype(BF16)
        out[:, CHUNK:] = dot(rows, held, 1, 1).astype(BF16)
        for r, ref in enumerate((g0, g1, g2, g3)):
            picked[block_rows(r), :CHUNK] = ref[:, chunk(place_ref, 0)]
            picked[block_rows(r), CHUNK:] = ref[:, chunk(place_ref, 1)]

    shape = (4 * TOK, WIDE)
    return call(body, [], [shape] * 2, [sds(shape)] * 2, place, (*grads, *couple))


def head_values(refs, own, other):
    query = jnp.concatenate([ref[0, :, own] for ref in refs[:4]], axis=0)
    cols = [own] * 4 + [other] * 4
    key = jnp.concatenate([ref[0, :, c] for ref, c in zip(refs[4:12], cols)], axis=0)
    value = jnp.concatenate([ref[1, :, c] for ref, c in zip(refs[4:12], cols)], axis=0)
    return query, key, value


def raised_scores(query, key):
    scores = dot(query, key, 1, 1)
    base = FACTOR * math.log2(math.e)
    return jnp.exp2(scores * base - jnp.max(scores, axis=-1, keepdims=True) * base)


def head_cols(j):
    return pl.ds(pl.multiple_of(j * HEAD, HEAD), HEAD)


def forward_partial(place, heads, inputs, proj):
    def body(place_ref, *refs):
        own_in, (own_w, mine, other), outs = refs[12:16], refs[16:19], refs[19:23]
        attended = refs[23]

        def two_heads(half, carry):
            for h in range(2):
                cols = head_cols(2 * half + h)
                query, key, value = head_values(refs, cols, head_cols(2 * (1 - half) + h))
                raised = raised_scores(query, key)
                total = jnp.sum(raised, axis=-1, keepdims=True)
                result = dot(raised.astype(BF16), value, 1, 0) / total
                attended[:, cols] = result.astype(BF16)
            return carry

        lax.fori_loop(0, 2, two_heads, 0)
        first, second = attended[:, :CHUNK], attended[:, CHUNK:]
        for rel in range(8):
            dest, half = rel >> 1, rel & 1
            cols = chunk(place_ref, rel)
            part = dot(first, own_w[:, cols], 1, 0)
            part = part + dot(second, held_rows(place_ref, mine, other, cols), 1, 0)
            at = slice(half * CHUNK, (half + 1) * CHUNK)
            for r in range(4):
                block = part[block_rows(r)]
                if dest == 0:
                    block = block + own_in[r][0, :, at].astype(F32)
                outs[dest][block_rows(r ^ dest), at] = block.astype(outs[dest].dtype)

    shape = (4 * TOK, WIDE)
    return call(
        body,
        [],
        [shape] * 4,
        [sds(shape, F32)] + [sds(shape)] * 3,
        place,
        (*heads, *inputs, *proj),
        scratch=[pltpu.VMEM(shape, BF16)],
    )


def mixed_partial(place, partner_hidden, hidden, couple):
    def body(place_ref, other_hid, own_hid, own_w, mine, other, *outs):
        first, second = other_hid[:, :CHUNK], other_hid[:, CHUNK:]
        for rel in range(8):
            cols = chunk(place_ref, rel)
            part = dot(first, own_w[:, cols], 1, 0)
            part = part + dot(second, held_rows(place_ref, mine, other, cols), 1, 0)
            if rel < 2:
                part = part + own_hid[:, rel * CHUNK : (rel + 1) * CHUNK].astype(F32)
            for r in range(4):
                outs[r][:, cols] = part[block_rows(r)].astype(outs[r].dtype)

    shape = (TOK, 8 * CHUNK)
    return call(
        body,
        [],
        [shape] * 4,
        [sds(shape, F32)] + [sds(shape)] * 3,
        place,
        (partner_hidden, hidden, *couple),
    )


def couple_gradient(place, partner_hidden, grads):
    def body(place_ref, hid, g0, g1, g2, g3, own, other):
        rows = stacked((g0, g1, g2, g3))
        other[...] = dot(hid[:, CHUNK:], rows, 0, 0).astype(BF16)
        own[...] = dot(hid[:, :CHUNK], rows, 0, 0)

    shape = (CHUNK, 8 * CHUNK)
    return call(
        body,
        [],
        [shape] * 2,
        [sds(shape, F32), sds(shape)],
        place,
        (partner_hidden, *grads),
    )


def backward_half(place, heads, grad_chunks, proj_rows, half):
    count = len(proj_rows)

    def body(place_ref, *refs):
        chunks, weights = refs[12:16], refs[16 : 16 + count]
        dq_out, kv_own, kv_other, grads = refs[16 + count :]
        grad_att = None
        for d, ref in enumerate(chunks):
            rows = jnp.concatenate([ref[block_rows(r ^ d)] for r in range(4)], axis=0)
            for h in range(2):
                cols = chunk(place_ref, 2 * d + h)
                if count == 1:
                    weight = weights[0][:, cols]
                else:
                    weight = held_rows(place_ref, *weights, cols)
                term = dot(rows[:, h * CHUNK : (h + 1) * CHUNK], weight, 1, 1)
                grad_att = term if grad_att is None else grad_att + term
        grads[...] = grad_att.astype(BF16)
        rows = 4 * TOK

        def one_head(j, carry):
            cols = head_cols(j)
            grad = grads[:, cols]
            query, key, value = head_values(refs, cols, cols)
            raised = raised_scores(query, key)
            weight = raised * (1.0 / jnp.sum(raised, axis=-1, keepdims=True))
            grad_weight = dot(grad, value, 1, 1)
            row_dot = jnp.sum(weight * grad_weight, axis=-1, keepdims=True)
            d_scores = (weight * (grad_weight - row_dot)).astype(BF16)
            dq_out[:, cols] = (dot(d_scores, key, 1, 0) * FACTOR).astype(BF16)
            d_key = (dot(d_scores, query, 0, 0) * FACTOR).astype(BF16)
            d_value = dot(weight.astype(BF16), grad, 0, 0).astype(BF16)
            kv_own[0, :, cols] = d_key[:rows]
            kv_own[1, :, cols] = d_value[:rows]
            kv_other[0, :, cols] = d_key[rows:]
            kv_other[1, :, cols] = d_value[rows:]
            return carry

        lax.fori_loop(0, 2, one_head, 0)

    def side(lead, at):
        return pl.BlockSpec((lead, TOK, CHUNK), lambda i, place: (0, 0, at))

    specs = [side(1, half)] * 4 + [side(2, half)] * 4 + [side(2, 1 - half)] * 4
    pair = (2, 4 * TOK, CHUNK)
    return call(
        body,
        specs,
        [(4 * TOK, CHUNK), pair, pair],
        [sds((4 * TOK, CHUNK)), sds(pair), sds(pair)],
        place,
        (*heads, *grad_chunks, *proj_rows),
        scratch=[pltpu.VMEM((4 * TOK, CHUNK), BF16)],
    )


def add_key_grads(place, own, other, query_grads):
    count = 2 + len(query_grads)

    def body(place_ref, a, b, *refs):
        ins, outs = refs[: count - 2], refs[count - 2 :]
        for r, out in enumerate(outs):
            rows = block_rows(r)
            for t in range(2):
                out[t] = (a[t, rows].astype(F32) + b[t, rows].astype(F32)).astype(BF16)
            for t, ref in enumerate(ins):
                out[2 + t] = ref[rows]

    shape = (count, TOK, CHUNK)
    return call(
        body, [], [shape] * 4, [sds(shape)] * 4, place, (own, other, *query_grads)
    )


def gradient_columns(place, low, high):
    def body(place_ref, *refs):
        lows, highs, (q_out, k_out, v_out) = refs[:4], refs[4:8], refs[8:]
        for r in range(4):
            even, odd = chunk(place_ref, 2 * r), chunk(place_ref, 2 * r + 1)
            q_out[:, even] = highs[r][2]
            q_out[:, odd] = highs[r][3]
            k_out[:, even] = lows[r][0]
            k_out[:, odd] = highs[r][0]
            v_out[:, even] = lows[r][1]
            v_out[:, odd] = highs[r][1]

    shape = (TOK, 8 * CHUNK)
    return call(body, [], [shape] * 3, [sds(shape)] * 3, place, (*low, *high))


def grad_hidden_columns(place, chunks):
    def body(place_ref, c0, c1, c2, c3, out):
        for r, ref in enumerate((c0, c1, c2, c3)):
            out[:, chunk(place_ref, 2 * r)] = ref[:, :CHUNK]
            out[:, chunk(place_ref, 2 * r + 1)] = ref[:, CHUNK:]

    specs = [pl.BlockSpec((TOK, WIDE), lambda i, place, r=r: (r, 0)) for r in range(4)]
    shape = (TOK, 8 * CHUNK)
    return call(body, specs, [shape], [sds(shape)], place, chunks)[0]


def exchange(pieces):
    got = [pieces[0], None, None, None]
    for r in (2, 1, 3):
        got[r] = seq_shift(pieces[r], 2 * r)
    return got


def steps(queries, key_vecs, value_vecs, hidden_in, out_proj, couple_proj, grad_mixed):
    odd_rep = lax.axis_index("rep").astype(jnp.int32) & 1
    place = jnp.stack([lax.axis_index("seq").astype(jnp.int32), odd_rep])
    pairs = relative_columns(place, (key_vecs[0], value_vecs[0]))
    pairs = exchange(pairs)
    others = [seq_shift(pairs[r], 1) for r in range(4)]
    couple_half = rep_shift(half_rows(couple_proj[0], odd_rep), 1)
    proj_half = rep_shift(half_rows(out_proj[0], odd_rep), 1)
    grads = exchange([grad_mixed[0]] * 4)
    items = exchange(relative_columns(place, (queries[0],)))
    inputs = exchange(relative_columns(place, (hidden_in[0],)))
    couple = (couple_proj[0], couple_half, rep_shift(couple_half, 0))
    proj = (out_proj[0], proj_half, rep_shift(proj_half, 0))
    heads = (*items, *pairs, *others)

    back, picked = back_couple_product(place, grads, couple)
    partner_back = branch_swap(back)
    total = (picked.astype(F32) + partner_back.astype(F32)).astype(BF16)
    chunks = exchange([total] * 4)

    sums = exchange(forward_partial(place, heads, inputs, proj))

    first = backward_half(place, heads, chunks, proj[:1], 0)
    got_high = seq_shift(first[2], 1)
    second = backward_half(place, heads, chunks, proj[1:], 1)
    got_low = seq_shift(second[2], 1)

    hidden = sums[0]
    for part in sums[1:]:
        hidden = hidden + part.astype(F32)
    hidden = hidden.astype(BF16)
    partner_hidden = branch_swap(hidden)
    mixed_parts = exchange(mixed_partial(place, partner_hidden, hidden, couple))
    couple_own, couple_other = couple_gradient(place, partner_hidden, grads)
    couple_got = seq_shift(couple_other, 1)

    high = add_key_grads(place, second[1], got_high, (first[0], second[0]))
    high = exchange(high)
    low = exchange(add_key_grads(place, first[1], got_low, ()))

    grad_hid = grad_hidden_columns(place, chunks)
    mixed = mixed_parts[0]
    for part in mixed_parts[1:]:
        mixed = mixed + part.astype(F32)
    grad_cpl = couple_own + couple_got.astype(F32)
    grad_q, grad_k, grad_v = gradient_columns(place, low, high)
    return (
        mixed.astype(BF16)[None],
        grad_hid[None],
        grad_q[None],
        grad_k[None],
        grad_v[None],
        grad_cpl[None],
    )


def solution(mesh):
    return jax.shard_map(
        steps,
        mesh=mesh,
        in_specs=(
            P("branch", ("rep", "seq"), None),
            P("branch", ("rep", "seq"), None),
            P("branch", ("rep", "seq"), None),
            P("branch", ("rep", "seq"), None),
            P("branch", "seq", None),
            P("branch", "seq", None),
            P("branch", ("rep", "seq"), None),
        ),
        out_specs=(
            P("branch", ("rep", "seq"), None),
            P("branch", ("rep", "seq"), None),
            P("branch", ("rep", "seq"), None),
            P("branch", ("rep", "seq"), None),
            P("branch", ("rep", "seq"), None),
            P("branch", "seq", "rep"),
        ),
        check_vma=False,
    )
```

profile of v0, /device:TPU:32, one launch (start us, length us, event | category | flops | bytes accessed | tf_op | source)
XLA Modules:
  0.0 229.0 jit_solution(1959701497594097106)
XLA Ops:
  1.9 2.8 %collective-permute-start.19 = (bf16[128,2048]{1,0:T(8,128)(2,1)S(1)}, bf16[128,2048]{1,0:T(8,128)(2,1)S(1)}, u32[]{:S(2)}, u32[]{:S(2)}) collective-permute-start(bf16[128,2048]{1,0:T(8,128)(2,1)S(1)} %dynamic-slice_bitcast_fusion), channel_id=1, source_target_pairs={{0,17},{1,16},{2,19},{3,18},{4,21},{5,20},{6,23},{7,22},{8,25},{9,... | collective-permute-start | bytes 1572872 | tf_op jit(solution)/shard_map/ppermute | solution.py:35
  9.4 2.9 %collective-permute-start.1 = (bf16[1,128,512]{2,1,0:T(8,128)(2,1)}, bf16[1,128,512]{2,1,0:T(8,128)(2,1)S(1)}, u32[]{:S(2)}, u32[]{:S(2)}) collective-permute-start(bf16[1,128,512]{2,1,0:T(8,128)(2,1)} %get-tuple-element.49), channel_id=1, source_target_pairs={{0,64},{16,80},{32,96},{48,112},{64,0},{80,16},{96,32},{112,48},{1... | collective-permute-start | bytes 393224 | tf_op jit(solution)/shard_map/ppermute | solution.py:23
  15.5 4.1 %collective-permute-start.11 = (bf16[1,128,512]{2,1,0:T(8,128)(2,1)}, bf16[1,128,512]{2,1,0:T(8,128)(2,1)S(1)}, u32[]{:S(2)}, u32[]{:S(2)}) collective-permute-start(bf16[1,128,512]{2,1,0:T(8,128)(2,1)} %get-tuple-element.57), channel_id=1, source_target_pairs={{0,64},{16,80},{32,96},{48,112},{64,0},{80,16},{96,32},{112,48},{1... | collective-permute-start | bytes 393224 | tf_op jit(solution)/shard_map/ppermute | solution.py:23
  21.4 4.8 %collective-permute-done.11.refs_14_ = bf16[1,128,512]{2,1,0:T(8,128)(2,1)S(1)} collective-permute-done((bf16[1,128,512]{2,1,0:T(8,128)(2,1)}, bf16[1,128,512]{2,1,0:T(8,128)(2,1)S(1)}, u32[]{:S(2)}, u32[]{:S(2)}) %collective-permute-start.11) | collective-permute-done | bytes 131104 | tf_op jit(solution)/shard_map/ppermute | solution.py:23
  28.7 3.0 %shard_map.119 = (bf16[2,128,512]{2,1,0:T(8,128)(2,1)}, bf16[2,128,512]{2,1,0:T(8,128)(2,1)}, bf16[2,128,512]{2,1,0:T(8,128)(2,1)}, bf16[2,128,512]{2,1,0:T(8,128)(2,1)}) custom-call(s32[2]{0:T(128)} %pad_add_fusion.place_ref, bf16[128,2048]{1,0:T(8,128)(2,1)} %bitcast.32, bf16[128,2048]{1,0:T(8,128)(2,1)} %bitcast.33), custom_call_target="tpu_custom_call" | custom-call | tf_op jit(solution)/shard_map/pallas_call | solution.py:54
  31.7 2.9 %collective-permute-done.13.refs_17_.refs_16_ = bf16[128,2048]{1,0:T(8,128)(2,1)S(1)} collective-permute-done((bf16[128,2048]{1,0:T(8,128)(2,1)S(1)}, bf16[128,2048]{1,0:T(8,128)(2,1)S(1)}, u32[]{:S(2)}, u32[]{:S(2)}) %collective-permute-start.13) | collective-permute-done | bytes 524320 | tf_op jit(solution)/shard_map/ppermute | solution.py:35
  38.5 11.0 %collective-permute-done.25.g2 = bf16[128,2048]{1,0:T(8,128)(2,1)S(1)} collective-permute-done((bf16[128,2048]{1,0:T(8,128)(2,1)S(1)}, bf16[128,2048]{1,0:T(8,128)(2,1)S(1)}, u32[]{:S(2)}, u32[]{:S(2)}) %collective-permute-start.25) | collective-permute-done | bytes 524320 | tf_op jit(solution)/shard_map/ppermute | solution.py:23
  50.1 6.0 %collective-permute-done.26.g3 = bf16[128,2048]{1,0:T(8,128)(2,1)S(1)} collective-permute-done((bf16[128,2048]{1,0:T(8,128)(2,1)S(1)}, bf16[128,2048]{1,0:T(8,128)(2,1)S(1)}, u32[]{:S(2)}, u32[]{:S(2)}) %collective-permute-start.26) | collective-permute-done | bytes 524320 | tf_op jit(solution)/shard_map/ppermute | solution.py:23
  57.2 5.1 %shard_map.123 = (bf16[512,512]{1,0:T(8,128)(2,1)}, bf16[512,512]{1,0:T(8,128)(2,1)}) custom-call(s32[2]{0:T(128)} %pad_add_fusion.place_ref, bf16[128,2048]{1,0:T(8,128)(2,1)} %bitcast.25, bf16[128,2048]{1,0:T(8,128)(2,1)} %copy-done.15, bf16[128,2048]{1,0:T(8,128)(2,1)} %copy-done.16, bf16[128,2048]{1,0:T(8,128)(2,1)} %copy-done.17, ...), custom_call_target="tpu_custom_call" | custom-call | tf_op jit(solution)/shard_map/pallas_call | solution.py:54
  62.5 3.4 %collective-permute-start.7 = (bf16[2,128,512]{2,1,0:T(8,128)(2,1)S(1)}, bf16[2,128,512]{2,1,0:T(8,128)(2,1)S(1)}, u32[]{:S(2)}, u32[]{:S(2)}) collective-permute-start(bf16[2,128,512]{2,1,0:T(8,128)(2,1)S(1)} %collective-permute-done.3.refs_5_), channel_id=1, source_target_pairs={{0,16},{16,0},{32,48},{48,32},{64,80},{80,64},{96,112},{112,96},{1... | collective-permute-start | bytes 786440 | tf_op jit(solution)/shard_map/ppermute | solution.py:23
  66.2 3.2 %collective-permute-start.9 = (bf16[2,128,512]{2,1,0:T(8,128)(2,1)S(1)}, bf16[2,128,512]{2,1,0:T(8,128)(2,1)S(1)}, u32[]{:S(2)}, u32[]{:S(2)}) collective-permute-start(bf16[2,128,512]{2,1,0:T(8,128)(2,1)S(1)} %collective-permute-done.5.refs_7_), channel_id=1, source_target_pairs={{0,16},{16,0},{32,48},{48,32},{64,80},{80,64},{96,112},{112,96},{1... | collective-permute-start | bytes 786440 | tf_op jit(solution)/shard_map/ppermute | solution.py:23
  69.5 8.6 %collective-permute-done.7.refs_9_ = bf16[2,128,512]{2,1,0:T(8,128)(2,1)S(1)} collective-permute-done((bf16[2,128,512]{2,1,0:T(8,128)(2,1)S(1)}, bf16[2,128,512]{2,1,0:T(8,128)(2,1)S(1)}, u32[]{:S(2)}, u32[]{:S(2)}) %collective-permute-start.7) | collective-permute-done | bytes 262176 | tf_op jit(solution)/shard_map/ppermute | solution.py:23
  78.0 5.6 %collective-permute-done.8.refs_10_ = bf16[2,128,512]{2,1,0:T(8,128)(2,1)S(1)} collective-permute-done((bf16[2,128,512]{2,1,0:T(8,128)(2,1)S(1)}, bf16[2,128,512]{2,1,0:T(8,128)(2,1)S(1)}, u32[]{:S(2)}, u32[]{:S(2)}) %collective-permute-start.8) | collective-permute-done | bytes 262176 | tf_op jit(solution)/shard_map/ppermute | solution.py:23
  83.7 3.0 %collective-permute-done.9.refs_11_ = bf16[2,128,512]{2,1,0:T(8,128)(2,1)S(1)} collective-permute-done((bf16[2,128,512]{2,1,0:T(8,128)(2,1)S(1)}, bf16[2,128,512]{2,1,0:T(8,128)(2,1)S(1)}, u32[]{:S(2)}, u32[]{:S(2)}) %collective-permute-start.9) | collective-permute-done | bytes 262176 | tf_op jit(solution)/shard_map/ppermute | solution.py:23
  87.5 9.8 %shard_map.121 = (f32[512,512]{1,0:T(8,128)}, bf16[512,512]{1,0:T(8,128)(2,1)}, bf16[512,512]{1,0:T(8,128)(2,1)}, bf16[512,512]{1,0:T(8,128)(2,1)}) custom-call(s32[2]{0:T(128)} %pad_add_fusion.place_ref, bf16[1,128,512]{2,1,0:T(8,128)(2,1)} %get-tuple-element.47.refs_0_, bf16[1,128,512]{2,1,0:T(8,128)(2,1)} %copy-done.23, bf16[1,128,512]{2,1,0:T(8,128)(2,1)} %copy-done.24, ...), custom_call_target="tpu_custom_call" | custom-call | tf_op jit(solution)/shard_map/pallas_call | solution.py:54
  97.4 3.9 %collective-permute-start.17 = (bf16[512,512]{1,0:T(8,128)(2,1)}, bf16[512,512]{1,0:T(8,128)(2,1)S(1)}, u32[]{:S(2)}, u32[]{:S(2)}) collective-permute-start(bf16[512,512]{1,0:T(8,128)(2,1)} %get-tuple-element.62), channel_id=1, source_target_pairs={{0,96},{16,112},{32,64},{48,80},{64,32},{80,48},{96,0},{112,16},{1... | collective-permute-start | bytes 1572872 | tf_op jit(solution)/shard_map/ppermute | solution.py:23
  103.6 3.5 %collective-permute-start.29 = (bf16[512,512]{1,0:T(8,128)(2,1)S(1)}, bf16[512,512]{1,0:T(8,128)(2,1)S(1)}, u32[]{:S(2)}, u32[]{:S(2)}) collective-permute-start(bf16[512,512]{1,0:T(8,128)(2,1)S(1)} %add_convert_fusion.c0.refs_12_), channel_id=1, source_target_pairs={{0,64},{16,80},{32,96},{48,112},{64,0},{80,16},{96,32},{112,48},{1... | collective-permute-start | bytes 1572872 | tf_op jit(solution)/shard_map/ppermute | solution.py:23
  107.1 15.2 %collective-permute-done.17 = bf16[512,512]{1,0:T(8,128)(2,1)S(1)} collective-permute-done((bf16[512,512]{1,0:T(8,128)(2,1)}, bf16[512,512]{1,0:T(8,128)(2,1)S(1)}, u32[]{:S(2)}, u32[]{:S(2)}) %collective-permute-start.17) | collective-permute-done | bytes 524320 | tf_op jit(solution)/shard_map/ppermute | solution.py:23
  122.3 3.0 %collective-permute-start.30 = (bf16[512,512]{1,0:T(8,128)(2,1)S(1)}, bf16[512,512]{1,0:T(8,128)(2,1)S(1)}, u32[]{:S(2)}, u32[]{:S(2)}) collective-permute-start(bf16[512,512]{1,0:T(8,128)(2,1)S(1)} %add_convert_fusion.c0.refs_12_), channel_id=1, source_target_pairs={{0,96},{16,112},{32,64},{48,80},{64,32},{80,48},{96,0},{112,16},{1... | collective-permute-start | bytes 1572872 | tf_op jit(solution)/shard_map/ppermute | solution.py:23
  126.9 10.8 %collective-permute-done.28.c1.refs_13_ = bf16[512,512]{1,0:T(8,128)(2,1)S(1)} collective-permute-done((bf16[512,512]{1,0:T(8,128)(2,1)S(1)}, bf16[512,512]{1,0:T(8,128)(2,1)S(1)}, u32[]{:S(2)}, u32[]{:S(2)}) %collective-permute-start.28) | collective-permute-done | bytes 524320 | tf_op jit(solution)/shard_map/ppermute | solution.py:23
  137.7 10.2 %collective-permute-done.29.c2.refs_14_ = bf16[512,512]{1,0:T(8,128)(2,1)S(1)} collective-permute-done((bf16[512,512]{1,0:T(8,128)(2,1)S(1)}, bf16[512,512]{1,0:T(8,128)(2,1)S(1)}, u32[]{:S(2)}, u32[]{:S(2)}) %collective-permute-start.29) | collective-permute-done | bytes 524320 | tf_op jit(solution)/shard_map/ppermute | solution.py:23
  149.5 8.9 %shard_map.126 = (bf16[512,256]{1,0:T(8,128)(2,1)}, bf16[2,512,256]{2,1,0:T(8,128)(2,1)}, bf16[2,512,256]{2,1,0:T(8,128)(2,1)}) custom-call(s32[2]{0:T(128)} %pad_add_fusion.place_ref, bf16[1,128,512]{2,1,0:T(8,128)(2,1)} %get-tuple-element.47.refs_0_, bf16[1,128,512]{2,1,0:T(8,128)(2,1)} %copy-done.23, bf16[1,128,512]{2,1,0:T(8,128)(2,1)} %copy-done.24, ...), custom_call_target="tpu_custom_call" | custom-call | tf_op jit(solution)/shard_map/pallas_call | solution.py:54
  161.9 5.2 %shard_map.122 = (f32[128,2048]{1,0:T(8,128)}, bf16[128,2048]{1,0:T(8,128)(2,1)}, bf16[128,2048]{1,0:T(8,128)(2,1)}, bf16[128,2048]{1,0:T(8,128)(2,1)}) custom-call(s32[2]{0:T(128)} %pad_add_fusion.place_ref, bf16[512,512]{1,0:T(8,128)(2,1)} %copy-done.21, bf16[512,512]{1,0:T(8,128)(2,1)} %copy-done.22, bf16[256,2048]{1,0:T(8,128)(2,1)} %bitcast.22, ...), custom_call_target="tpu_custom_call" | custom-call | tf_op jit(solution)/shard_map/pallas_call | solution.py:54
  169.6 8.9 %shard_map.125 = (bf16[512,256]{1,0:T(8,128)(2,1)}, bf16[2,512,256]{2,1,0:T(8,128)(2,1)}, bf16[2,512,256]{2,1,0:T(8,128)(2,1)}) custom-call(s32[2]{0:T(128)} %pad_add_fusion.place_ref, bf16[1,128,512]{2,1,0:T(8,128)(2,1)} %get-tuple-element.47.refs_0_, bf16[1,128,512]{2,1,0:T(8,128)(2,1)} %copy-done.23, bf16[1,128,512]{2,1,0:T(8,128)(2,1)} %copy-done.24, ...), custom_call_target="tpu_custom_call" | custom-call | tf_op jit(solution)/shard_map/pallas_call | solution.py:54
  181.0 4.9 %shard_map.130 = (f32[256,2048]{1,0:T(8,128)}, bf16[256,2048]{1,0:T(8,128)(2,1)}) custom-call(s32[2]{0:T(128)} %pad_add_fusion.place_ref, bf16[512,512]{1,0:T(8,128)(2,1)} %copy-done.21, bf16[128,2048]{1,0:T(8,128)(2,1)} %bitcast.26, bf16[128,2048]{1,0:T(8,128)(2,1)} %copy-done.15, bf16[128,2048]{1,0:T(8,128)(2,1)} %copy-done.16, bf16[128,2048]{1,0:T(8,128)(2,1)} %copy-done.17), custom_call_target="tpu_custom_call" | custom-call | tf_op jit(solution)/shard_map/pallas_call | solution.py:54
  185.9 2.8 %collective-permute-start.39 = (bf16[256,2048]{1,0:T(8,128)(2,1)}, bf16[256,2048]{1,0:T(8,128)(2,1)S(1)}, u32[]{:S(2)}, u32[]{:S(2)}) collective-permute-start(bf16[256,2048]{1,0:T(8,128)(2,1)} %get-tuple-element.87), channel_id=1, source_target_pairs={{0,16},{16,0},{32,48},{48,32},{64,80},{80,64},{96,112},{112,96},{1... | collective-permute-start | bytes 3145736 | tf_op jit(solution)/shard_map/ppermute | solution.py:23
  191.9 3.1 %collective-permute-done.35.b = bf16[2,512,256]{2,1,0:T(8,128)(2,1)S(1)} collective-permute-done((bf16[2,512,256]{2,1,0:T(8,128)(2,1)}, bf16[2,512,256]{2,1,0:T(8,128)(2,1)S(1)}, u32[]{:S(2)}, u32[]{:S(2)}) %collective-permute-start.35) | collective-permute-done | bytes 524320 | tf_op jit(solution)/shard_map/ppermute | solution.py:23
  198.2 3.0 %shard_map.128 = (bf16[4,128,256]{2,1,0:T(8,128)(2,1)}, bf16[4,128,256]{2,1,0:T(8,128)(2,1)}, bf16[4,128,256]{2,1,0:T(8,128)(2,1)}, bf16[4,128,256]{2,1,0:T(8,128)(2,1)}) custom-call(s32[2]{0:T(128)} %pad_add_fusion.place_ref, bf16[2,512,256]{2,1,0:T(8,128)(2,1)} %get-tuple-element.75.a, bf16[2,512,256]{2,1,0:T(8,128)(2,1)} %copy-done.29, ...), custom_call_target="tpu_custom_call" | custom-call | tf_op jit(solution)/shard_map/pallas_call | solution.py:54
  201.9 3.0 %collective-permute-done.21 = bf16[128,2048]{1,0:T(8,128)(2,1)S(1)} collective-permute-done((bf16[128,2048]{1,0:T(8,128)(2,1)S(1)}, bf16[128,2048]{1,0:T(8,128)(2,1)S(1)}, u32[]{:S(2)}, u32[]{:S(2)}) %collective-permute-start.21) | collective-permute-done | bytes 524320 | tf_op jit(solution)/shard_map/ppermute | solution.py:23
  209.4 3.3 %collective-permute-done.33.refs_2_ = bf16[2,128,256]{2,1,0:T(8,128)(2,1)S(1)} collective-permute-done((bf16[2,128,256]{2,1,0:T(8,128)(2,1)}, bf16[2,128,256]{2,1,0:T(8,128)(2,1)S(1)}, u32[]{:S(2)}, u32[]{:S(2)}) %collective-permute-start.33) | collective-permute-done | bytes 131104 | tf_op jit(solution)/shard_map/ppermute | solution.py:23
  215.8 5.0 %collective-permute-done.37.refs_6_ = bf16[4,128,256]{2,1,0:T(8,128)(2,1)S(1)} collective-permute-done((bf16[4,128,256]{2,1,0:T(8,128)(2,1)}, bf16[4,128,256]{2,1,0:T(8,128)(2,1)S(1)}, u32[]{:S(2)}, u32[]{:S(2)}) %collective-permute-start.37) | collective-permute-done | bytes 262176 | tf_op jit(solution)/shard_map/ppermute | solution.py:23
  224.0 3.4 %shard_map.129 = (bf16[128,2048]{1,0:T(8,128)(2,1)}, bf16[128,2048]{1,0:T(8,128)(2,1)}, bf16[128,2048]{1,0:T(8,128)(2,1)}) custom-call(s32[2]{0:T(128)} %pad_add_fusion.place_ref, bf16[2,128,256]{2,1,0:T(8,128)(2,1)} %get-tuple-element.71.refs_0_, bf16[2,128,256]{2,1,0:T(8,128)(2,1)} %copy-done.37, bf16[2,128,256]{2,1,0:T(8,128)(2,1)} %copy-done.38, ...), custom_call_target="tpu_custom_call" | custom-call | tf_op jit(solution)/shard_map/pallas_call | solution.py:54
  (154 shorter events, 53.8 us)
Async XLA Ops:
  1.9 26.7 %collective-permute-start.19 = (bf16[128,2048]{1,0:T(8,128)(2,1)S(1)}, bf16[128,2048]{1,0:T(8,128)(2,1)S(1)}, u32[]{:S(2)}, u32[]{:S(2)}) collective-permute-start(bf16[128,2048]{1,0:T(8,128)(2,1)S(1)} %dynamic-slice_bitcast_fusion), channel_id=1, source_target_pairs={{0,17},{1,16},{2,19},{3,18},{4,21},{5,20},{6,23},{7,22},{8,25},{9,... | collective-permute-start | bytes 1572872 | tf_op jit(solution)/shard_map/ppermute | solution.py:35
  20.3 14.3 %collective-permute-start.13 = (bf16[128,2048]{1,0:T(8,128)(2,1)S(1)}, bf16[128,2048]{1,0:T(8,128)(2,1)S(1)}, u32[]{:S(2)}, u32[]{:S(2)}) collective-permute-start(bf16[128,2048]{1,0:T(8,128)(2,1)S(1)} %dynamic-slice_bitcast_fusion.1), channel_id=1, source_target_pairs={{0,17},{1,16},{2,19},{3,18},{4,21},{5,20},{6,23},{7,22},{8,25},{9,... | collective-permute-start | bytes 1572872 | tf_op jit(solution)/shard_map/ppermute | solution.py:35
  21.4 14.8 %collective-permute-start.24 = (bf16[128,2048]{1,0:T(8,128)(2,1)S(1)}, bf16[128,2048]{1,0:T(8,128)(2,1)S(1)}, u32[]{:S(2)}, u32[]{:S(2)}) collective-permute-start(bf16[128,2048]{1,0:T(8,128)(2,1)S(1)} %bitcast.27), channel_id=1, source_target_pairs={{0,32},{16,48},{32,0},{48,16},{64,96},{80,112},{96,64},{112,80},{1... | collective-permute-start | bytes 1572872 | tf_op jit(solution)/shard_map/ppermute | solution.py:23
  26.2 23.3 %collective-permute-start.25 = (bf16[128,2048]{1,0:T(8,128)(2,1)S(1)}, bf16[128,2048]{1,0:T(8,128)(2,1)S(1)}, u32[]{:S(2)}, u32[]{:S(2)}) collective-permute-start(bf16[128,2048]{1,0:T(8,128)(2,1)S(1)} %bitcast.28), channel_id=1, source_target_pairs={{0,64},{16,80},{32,96},{48,112},{64,0},{80,16},{96,32},{112,48},{1... | collective-permute-start | bytes 1572872 | tf_op jit(solution)/shard_map/ppermute | solution.py:23
  27.7 28.4 %collective-permute-start.26 = (bf16[128,2048]{1,0:T(8,128)(2,1)S(1)}, bf16[128,2048]{1,0:T(8,128)(2,1)S(1)}, u32[]{:S(2)}, u32[]{:S(2)}) collective-permute-start(bf16[128,2048]{1,0:T(8,128)(2,1)S(1)} %bitcast.29), channel_id=1, source_target_pairs={{0,96},{16,112},{32,64},{48,80},{64,32},{80,48},{96,0},{112,16},{1... | collective-permute-start | bytes 1572872 | tf_op jit(solution)/shard_map/ppermute | solution.py:23
  28.6 27.8 %collective-permute-start.20 = (bf16[128,2048]{1,0:T(8,128)(2,1)S(1)}, bf16[128,2048]{1,0:T(8,128)(2,1)S(1)}, u32[]{:S(2)}, u32[]{:S(2)}) collective-permute-start(bf16[128,2048]{1,0:T(8,128)(2,1)S(1)} %collective-permute-done.19.mine), channel_id=1, source_target_pairs={{0,1},{1,0},{2,3},{3,2},{4,5},{5,4},{6,7},{7,6},{8,9},{9,8},{10,11... | collective-permute-start | bytes 1572872 | tf_op jit(solution)/shard_map/ppermute | solution.py:35
  34.6 27.8 %collective-permute-start.3 = (bf16[2,128,512]{2,1,0:T(8,128)(2,1)}, bf16[2,128,512]{2,1,0:T(8,128)(2,1)S(1)}, u32[]{:S(2)}, u32[]{:S(2)}) collective-permute-start(bf16[2,128,512]{2,1,0:T(8,128)(2,1)} %get-tuple-element.52), channel_id=1, source_target_pairs={{0,32},{16,48},{32,0},{48,16},{64,96},{80,112},{96,64},{112,80},{1... | collective-permute-start | bytes 786440 | tf_op jit(solution)/shard_map/ppermute | solution.py:23
  36.2 26.3 %collective-permute-start.4 = (bf16[2,128,512]{2,1,0:T(8,128)(2,1)}, bf16[2,128,512]{2,1,0:T(8,128)(2,1)S(1)}, u32[]{:S(2)}, u32[]{:S(2)}) collective-permute-start(bf16[2,128,512]{2,1,0:T(8,128)(2,1)} %get-tuple-element.53), channel_id=1, source_target_pairs={{0,64},{16,80},{32,96},{48,112},{64,0},{80,16},{96,32},{112,48},{1... | collective-permute-start | bytes 786440 | tf_op jit(solution)/shard_map/ppermute | solution.py:23
  49.5 16.4 %collective-permute-start.5 = (bf16[2,128,512]{2,1,0:T(8,128)(2,1)}, bf16[2,128,512]{2,1,0:T(8,128)(2,1)S(1)}, u32[]{:S(2)}, u32[]{:S(2)}) collective-permute-start(bf16[2,128,512]{2,1,0:T(8,128)(2,1)} %get-tuple-element.54), channel_id=1, source_target_pairs={{0,96},{16,112},{32,64},{48,80},{64,32},{80,48},{96,0},{112,16},{1... | collective-permute-start | bytes 786440 | tf_op jit(solution)/shard_map/ppermute | solution.py:23
  56.4 30.3 %collective-permute-start.14 = (bf16[128,2048]{1,0:T(8,128)(2,1)S(1)}, bf16[128,2048]{1,0:T(8,128)(2,1)S(1)}, u32[]{:S(2)}, u32[]{:S(2)}) collective-permute-start(bf16[128,2048]{1,0:T(8,128)(2,1)S(1)} %collective-permute-done.13.refs_17_.refs_16_), channel_id=1, source_target_pairs={{0,1},{1,0},{2,3},{3,2},{4,5},{5,4},{6,7},{7,6},{8,9},{9,8},{10,11... | collective-permute-start | bytes 1572872 | tf_op jit(solution)/shard_map/ppermute | solution.py:35
  62.4 39.9 %collective-permute-start.27 = (bf16[512,512]{1,0:T(8,128)(2,1)}, bf16[512,512]{1,0:T(8,128)(2,1)S(1)}, u32[]{:S(2)}, u32[]{:S(2)}) collective-permute-start(bf16[512,512]{1,0:T(8,128)(2,1)} %get-tuple-element.68), channel_id=1, source_target_pairs={{0,128},{128,0},{1,129},{129,1},{2,130},{130,2},{3,131},{131,3},{4... | collective-permute-start | bytes 1572872 | tf_op jit(solution)/shard_map/ppermute | solution.py:27
  62.5 15.6 %collective-permute-start.7 = (bf16[2,128,512]{2,1,0:T(8,128)(2,1)S(1)}, bf16[2,128,512]{2,1,0:T(8,128)(2,1)S(1)}, u32[]{:S(2)}, u32[]{:S(2)}) collective-permute-start(bf16[2,128,512]{2,1,0:T(8,128)(2,1)S(1)} %collective-permute-done.3.refs_5_), channel_id=1, source_target_pairs={{0,16},{16,0},{32,48},{48,32},{64,80},{80,64},{96,112},{112,96},{1... | collective-permute-start | bytes 786440 | tf_op jit(solution)/shard_map/ppermute | solution.py:23
  65.9 17.7 %collective-permute-start.8 = (bf16[2,128,512]{2,1,0:T(8,128)(2,1)S(1)}, bf16[2,128,512]{2,1,0:T(8,128)(2,1)S(1)}, u32[]{:S(2)}, u32[]{:S(2)}) collective-permute-start(bf16[2,128,512]{2,1,0:T(8,128)(2,1)S(1)} %collective-permute-done.4.refs_6_), channel_id=1, source_target_pairs={{0,16},{16,0},{32,48},{48,32},{64,80},{80,64},{96,112},{112,96},{1... | collective-permute-start | bytes 786440 | tf_op jit(solution)/shard_map/ppermute | solution.py:23
  66.2 20.4 %collective-permute-start.9 = (bf16[2,128,512]{2,1,0:T(8,128)(2,1)S(1)}, bf16[2,128,512]{2,1,0:T(8,128)(2,1)S(1)}, u32[]{:S(2)}, u32[]{:S(2)}) collective-permute-start(bf16[2,128,512]{2,1,0:T(8,128)(2,1)S(1)} %collective-permute-done.5.refs_7_), channel_id=1, source_target_pairs={{0,16},{16,0},{32,48},{48,32},{64,80},{80,64},{96,112},{112,96},{1... | collective-permute-start | bytes 786440 | tf_op jit(solution)/shard_map/ppermute | solution.py:23
  97.4 24.9 %collective-permute-start.17 = (bf16[512,512]{1,0:T(8,128)(2,1)}, bf16[512,512]{1,0:T(8,128)(2,1)S(1)}, u32[]{:S(2)}, u32[]{:S(2)}) collective-permute-start(bf16[512,512]{1,0:T(8,128)(2,1)} %get-tuple-element.62), channel_id=1, source_target_pairs={{0,96},{16,112},{32,64},{48,80},{64,32},{80,48},{96,0},{112,16},{1... | collective-permute-start | bytes 1572872 | tf_op jit(solution)/shard_map/ppermute | solution.py:23
  101.3 24.0 %collective-permute-start.16 = (bf16[512,512]{1,0:T(8,128)(2,1)}, bf16[512,512]{1,0:T(8,128)(2,1)S(1)}, u32[]{:S(2)}, u32[]{:S(2)}) collective-permute-start(bf16[512,512]{1,0:T(8,128)(2,1)} %get-tuple-element.61), channel_id=1, source_target_pairs={{0,64},{16,80},{32,96},{48,112},{64,0},{80,16},{96,32},{112,48},{1... | collective-permute-start | bytes 1572872 | tf_op jit(solution)/shard_map/ppermute | solution.py:23
  101.3 25.2 %collective-permute-start.15 = (bf16[512,512]{1,0:T(8,128)(2,1)}, bf16[512,512]{1,0:T(8,128)(2,1)S(1)}, u32[]{:S(2)}, u32[]{:S(2)}) collective-permute-start(bf16[512,512]{1,0:T(8,128)(2,1)} %get-tuple-element.60), channel_id=1, source_target_pairs={{0,32},{16,48},{32,0},{48,16},{64,96},{80,112},{96,64},{112,80},{1... | collective-permute-start | bytes 1572872 | tf_op jit(solution)/shard_map/ppermute | solution.py:23
  102.4 35.3 %collective-permute-start.28 = (bf16[512,512]{1,0:T(8,128)(2,1)S(1)}, bf16[512,512]{1,0:T(8,128)(2,1)S(1)}, u32[]{:S(2)}, u32[]{:S(2)}) collective-permute-start(bf16[512,512]{1,0:T(8,128)(2,1)S(1)} %add_convert_fusion.c0.refs_12_), channel_id=1, source_target_pairs={{0,32},{16,48},{32,0},{48,16},{64,96},{80,112},{96,64},{112,80},{1... | collective-permute-start | bytes 1572872 | tf_op jit(solution)/shard_map/ppermute | solution.py:23
  103.6 44.3 %collective-permute-start.29 = (bf16[512,512]{1,0:T(8,128)(2,1)S(1)}, bf16[512,512]{1,0:T(8,128)(2,1)S(1)}, u32[]{:S(2)}, u32[]{:S(2)}) collective-permute-start(bf16[512,512]{1,0:T(8,128)(2,1)S(1)} %add_convert_fusion.c0.refs_12_), channel_id=1, source_target_pairs={{0,64},{16,80},{32,96},{48,112},{64,0},{80,16},{96,32},{112,48},{1... | collective-permute-start | bytes 1572872 | tf_op jit(solution)/shard_map/ppermute | solution.py:23
  122.3 25.9 %collective-permute-start.30 = (bf16[512,512]{1,0:T(8,128)(2,1)S(1)}, bf16[512,512]{1,0:T(8,128)(2,1)S(1)}, u32[]{:S(2)}, u32[]{:S(2)}) collective-permute-start(bf16[512,512]{1,0:T(8,128)(2,1)S(1)} %add_convert_fusion.c0.refs_12_), channel_id=1, source_target_pairs={{0,96},{16,112},{32,64},{48,80},{64,32},{80,48},{96,0},{112,16},{1... | collective-permute-start | bytes 1572872 | tf_op jit(solution)/shard_map/ppermute | solution.py:23
  126.8 34.2 %collective-permute-start.18 = (bf16[512,512]{1,0:T(8,128)(2,1)S(1)}, bf16[512,512]{1,0:T(8,128)(2,1)S(1)}, u32[]{:S(2)}, u32[]{:S(2)}) collective-permute-start(bf16[512,512]{1,0:T(8,128)(2,1)S(1)} %add_convert_fusion.2.own_hid), channel_id=1, source_target_pairs={{0,128},{128,0},{1,129},{129,1},{2,130},{130,2},{3,131},{131,3},{4... | collective-permute-start | bytes 1572872 | tf_op jit(solution)/shard_map/ppermute | solution.py:27
  158.4 27.5 %collective-permute-start.31 = (bf16[2,512,256]{2,1,0:T(8,128)(2,1)}, bf16[2,512,256]{2,1,0:T(8,128)(2,1)S(1)}, u32[]{:S(2)}, u32[]{:S(2)}) collective-permute-start(bf16[2,512,256]{2,1,0:T(8,128)(2,1)} %get-tuple-element.70), channel_id=1, source_target_pairs={{0,16},{16,0},{32,48},{48,32},{64,80},{80,64},{96,112},{112,96},{1... | collective-permute-start | bytes 1572872 | tf_op jit(solution)/shard_map/ppermute | solution.py:23
  167.1 24.3 %collective-permute-start.23 = (bf16[128,2048]{1,0:T(8,128)(2,1)}, bf16[128,2048]{1,0:T(8,128)(2,1)S(1)}, u32[]{:S(2)}, u32[]{:S(2)}) collective-permute-start(bf16[128,2048]{1,0:T(8,128)(2,1)} %get-tuple-element.66), channel_id=1, source_target_pairs={{0,96},{16,112},{32,64},{48,80},{64,32},{80,48},{96,0},{112,16},{1... | collective-permute-start | bytes 1572872 | tf_op jit(solution)/shard_map/ppermute | solution.py:23
  178.5 16.5 %collective-permute-start.35 = (bf16[2,512,256]{2,1,0:T(8,128)(2,1)}, bf16[2,512,256]{2,1,0:T(8,128)(2,1)S(1)}, u32[]{:S(2)}, u32[]{:S(2)}) collective-permute-start(bf16[2,512,256]{2,1,0:T(8,128)(2,1)} %get-tuple-element.76), channel_id=1, source_target_pairs={{0,16},{16,0},{32,48},{48,32},{64,80},{80,64},{96,112},{112,96},{1... | collective-permute-start | bytes 1572872 | tf_op jit(solution)/shard_map/ppermute | solution.py:23
  179.4 21.8 %collective-permute-start.22 = (bf16[128,2048]{1,0:T(8,128)(2,1)S(1)}, bf16[128,2048]{1,0:T(8,128)(2,1)S(1)}, u32[]{:S(2)}, u32[]{:S(2)}) collective-permute-start(bf16[128,2048]{1,0:T(8,128)(2,1)S(1)} %copy-done.41), channel_id=1, source_target_pairs={{0,64},{16,80},{32,96},{48,112},{64,0},{80,16},{96,32},{112,48},{1... | collective-permute-start | bytes 1572872 | tf_op jit(solution)/shard_map/ppermute | solution.py:23
  179.4 25.6 %collective-permute-start.21 = (bf16[128,2048]{1,0:T(8,128)(2,1)S(1)}, bf16[128,2048]{1,0:T(8,128)(2,1)S(1)}, u32[]{:S(2)}, u32[]{:S(2)}) collective-permute-start(bf16[128,2048]{1,0:T(8,128)(2,1)S(1)} %copy-done.40), channel_id=1, source_target_pairs={{0,32},{16,48},{32,0},{48,16},{64,96},{80,112},{96,64},{112,80},{1... | collective-permute-start | bytes 1572872 | tf_op jit(solution)/shard_map/ppermute | solution.py:23
  185.9 41.4 %collective-permute-start.39 = (bf16[256,2048]{1,0:T(8,128)(2,1)}, bf16[256,2048]{1,0:T(8,128)(2,1)S(1)}, u32[]{:S(2)}, u32[]{:S(2)}) collective-permute-start(bf16[256,2048]{1,0:T(8,128)(2,1)} %get-tuple-element.87), channel_id=1, source_target_pairs={{0,16},{16,0},{32,48},{48,32},{64,80},{80,64},{96,112},{112,96},{1... | collective-permute-start | bytes 3145736 | tf_op jit(solution)/shard_map/ppermute | solution.py:23
  191.4 16.4 %collective-permute-start.32 = (bf16[2,128,256]{2,1,0:T(8,128)(2,1)}, bf16[2,128,256]{2,1,0:T(8,128)(2,1)S(1)}, u32[]{:S(2)}, u32[]{:S(2)}) collective-permute-start(bf16[2,128,256]{2,1,0:T(8,128)(2,1)} %get-tuple-element.72), channel_id=1, source_target_pairs={{0,32},{16,48},{32,0},{48,16},{64,96},{80,112},{96,64},{112,80},{1... | collective-permute-start | bytes 393224 | tf_op jit(solution)/shard_map/ppermute | solution.py:23
  195.0 17.6 %collective-permute-start.33 = (bf16[2,128,256]{2,1,0:T(8,128)(2,1)}, bf16[2,128,256]{2,1,0:T(8,128)(2,1)S(1)}, u32[]{:S(2)}, u32[]{:S(2)}) collective-permute-start(bf16[2,128,256]{2,1,0:T(8,128)(2,1)} %get-tuple-element.73), channel_id=1, source_target_pairs={{0,64},{16,80},{32,96},{48,112},{64,0},{80,16},{96,32},{112,48},{1... | collective-permute-start | bytes 393224 | tf_op jit(solution)/shard_map/ppermute | solution.py:23
  201.2 13.2 %collective-permute-start.34 = (bf16[2,128,256]{2,1,0:T(8,128)(2,1)S(1)}, bf16[2,128,256]{2,1,0:T(8,128)(2,1)S(1)}, u32[]{:S(2)}, u32[]{:S(2)}) collective-permute-start(bf16[2,128,256]{2,1,0:T(8,128)(2,1)S(1)} %copy-done.42), channel_id=1, source_target_pairs={{0,96},{16,112},{32,64},{48,80},{64,32},{80,48},{96,0},{112,16},{1... | collective-permute-start | bytes 393224 | tf_op jit(solution)/shard_map/ppermute | solution.py:23
  205.0 10.8 %collective-permute-start.36 = (bf16[4,128,256]{2,1,0:T(8,128)(2,1)}, bf16[4,128,256]{2,1,0:T(8,128)(2,1)S(1)}, u32[]{:S(2)}, u32[]{:S(2)}) collective-permute-start(bf16[4,128,256]{2,1,0:T(8,128)(2,1)} %get-tuple-element.80), channel_id=1, source_target_pairs={{0,32},{16,48},{32,0},{48,16},{64,96},{80,112},{96,64},{112,80},{1... | collective-permute-start | bytes 786440 | tf_op jit(solution)/shard_map/ppermute | solution.py:23
  207.8 12.9 %collective-permute-start.37 = (bf16[4,128,256]{2,1,0:T(8,128)(2,1)}, bf16[4,128,256]{2,1,0:T(8,128)(2,1)S(1)}, u32[]{:S(2)}, u32[]{:S(2)}) collective-permute-start(bf16[4,128,256]{2,1,0:T(8,128)(2,1)} %get-tuple-element.81), channel_id=1, source_target_pairs={{0,64},{16,80},{32,96},{48,112},{64,0},{80,16},{96,32},{112,48},{1... | collective-permute-start | bytes 786440 | tf_op jit(solution)/shard_map/ppermute | solution.py:23
  (51 other events, 818.5 us)
where the time goes:
time: 230 us; the launch traced here: 229 us
  waiting for transfers between devices  103 us (45%)
  Pallas kernels  62.8 us (27%)
  starting transfers between devices  53 us (23%)
  local copies, waits for them, and re-layouts  5.66 us (2%)
  other arithmetic  3.82 us (2%)
    ppermute x34, waiting for transfers between devices, seq_shift(): return lax.ppermute(value, 'seq', [(i, i ^ mask) for i in range(size)])  99.9 us
    pallas_call x13, Pallas kernels, call(): pl.pallas_call(body, out_shape=out_shapes, grid_spec=pltpu.PrefetchScalar...  62.8 us
    ppermute x34, starting transfers between devices, seq_shift(): return lax.ppermute(value, 'seq', [(i, i ^ mask) for i in range(size)])  49.3 us
  transfers between devices with their start and end apart: 40, of which 22 were waited for; matrix products, arithmetic and copies ran while one was open for 1% of the time, Pallas kernels for 27%

commit v1 on v0

--- a/solution.py
+++ b/solution.py
@@ -137,10 +137,9 @@
     return pl.ds(pl.multiple_of(j * HEAD, HEAD), HEAD)
 
 
-def forward_partial(place, heads, inputs, proj):
+def forward_partial(place, heads, proj):
     def body(place_ref, *refs):
-        own_in, (own_w, mine, other), outs = refs[12:16], refs[16:19], refs[19:23]
-        attended = refs[23]
+        (own_w, mine, other), outs, attended = refs[12:15], refs[15:19], refs[19]
 
         def two_heads(half, carry):
             for h in range(2):
@@ -161,10 +160,8 @@
             part = part + dot(second, held_rows(place_ref, mine, other, cols), 1, 0)
             at = slice(half * CHUNK, (half + 1) * CHUNK)
             for r in range(4):
-                block = part[block_rows(r)]
-                if dest == 0:
-                    block = block + own_in[r][0, :, at].astype(F32)
-                outs[dest][block_rows(r ^ dest), at] = block.astype(outs[dest].dtype)
+                block = part[block_rows(r)].astype(outs[dest].dtype)
+                outs[dest][block_rows(r ^ dest), at] = block
 
     shape = (4 * TOK, WIDE)
     return call(
@@ -173,7 +170,7 @@
         [shape] * 4,
         [sds(shape, F32)] + [sds(shape)] * 3,
         place,
-        (*heads, *inputs, *proj),
+        (*heads, *proj),
         scratch=[pltpu.VMEM(shape, BF16)],
     )
 
@@ -346,14 +343,14 @@
     total = (picked.astype(F32) + partner_back.astype(F32)).astype(BF16)
     chunks = exchange([total] * 4)
 
-    sums = exchange(forward_partial(place, heads, inputs, proj))
+    sums = exchange(forward_partial(place, heads, proj))
 
     first = backward_half(place, heads, chunks, proj[:1], 0)
     got_high = seq_shift(first[2], 1)
     second = backward_half(place, heads, chunks, proj[1:], 1)
     got_low = seq_shift(second[2], 1)
 
-    hidden = sums[0]
+    hidden = sums[0] + jnp.concatenate([block[0] for block in inputs]).astype(F32)
     for part in sums[1:]:
         hidden = hidden + part.astype(F32)
     hidden = hidden.astype(BF16)

time: 230 us -> 232 us (level)
  the two profiles are of different devices: /device:TPU:32 before, /device:TPU:2 now
where the time goes in v1:
time: 232 us
  waiting for transfers between devices  103 us (44%)
  Pallas kernels  62.5 us (27%)
  starting transfers between devices  55 us (24%)
  local copies, waits for them, and re-layouts  5.41 us (2%)
  other arithmetic  4.8 us (2%)
    ppermute x34, waiting for transfers between devices, seq_shift(): return lax.ppermute(value, 'seq', [(i, i ^ mask) for i in range(size)])  102 us
    pallas_call x13, Pallas kernels, call(): pl.pallas_call(body, out_shape=out_shapes, grid_spec=pltpu.PrefetchScalar...  62.5 us
    ppermute x34, starting transfers between devices, seq_shift(): return lax.ppermute(value, 'seq', [(i, i ^ mask) for i in range(size)])  48.2 us
    ppermute x4, starting transfers between devices, rep_shift(): return lax.ppermute(value, ('seq', 'rep'), pairs)  6.55 us
  transfers between devices with their start and end apart: 40, of which 18 were waited for; matrix products, arithmetic and copies ran while one was open for 2% of the time, Pallas kernels for 27%

profile of v1, /device:TPU:2, one launch (start us, length us, event | category | flops | bytes accessed | tf_op | source)
XLA Modules:
  0.0 231.6 jit_solution(11364642887648177899)
XLA Ops:
  4.0 2.6 %shard_map.118 = (bf16[1,128,512]{2,1,0:T(8,128)(2,1)}, bf16[1,128,512]{2,1,0:T(8,128)(2,1)}, bf16[1,128,512]{2,1,0:T(8,128)(2,1)}, bf16[1,128,512]{2,1,0:T(8,128)(2,1)}) custom-call(s32[2]{0:T(128)} %pad_add_fusion.place_ref, bf16[128,2048]{1,0:T(8,128)(2,1)} %bitcast.34), custom_call_target="tpu_custom_call" | custom-call | tf_op jit(solution)/shard_map/pallas_call | solution.py:54
  8.2 2.9 %collective-permute-start.1 = (bf16[1,128,512]{2,1,0:T(8,128)(2,1)}, bf16[1,128,512]{2,1,0:T(8,128)(2,1)S(1)}, u32[]{:S(2)}, u32[]{:S(2)}) collective-permute-start(bf16[1,128,512]{2,1,0:T(8,128)(2,1)} %get-tuple-element.49), channel_id=1, source_target_pairs={{0,64},{16,80},{32,96},{48,112},{64,0},{80,16},{96,32},{112,48},{1... | collective-permute-start | bytes 393224 | tf_op jit(solution)/shard_map/ppermute | solution.py:23
  13.5 3.9 %collective-permute-done.1.refs_2_ = bf16[1,128,512]{2,1,0:T(8,128)(2,1)S(1)} collective-permute-done((bf16[1,128,512]{2,1,0:T(8,128)(2,1)}, bf16[1,128,512]{2,1,0:T(8,128)(2,1)S(1)}, u32[]{:S(2)}, u32[]{:S(2)}) %collective-permute-start.1) | collective-permute-done | bytes 131104 | tf_op jit(solution)/shard_map/ppermute | solution.py:23
  22.6 3.0 %shard_map.119 = (bf16[2,128,512]{2,1,0:T(8,128)(2,1)}, bf16[2,128,512]{2,1,0:T(8,128)(2,1)}, bf16[2,128,512]{2,1,0:T(8,128)(2,1)}, bf16[2,128,512]{2,1,0:T(8,128)(2,1)}) custom-call(s32[2]{0:T(128)} %pad_add_fusion.place_ref, bf16[128,2048]{1,0:T(8,128)(2,1)} %bitcast.36, bf16[128,2048]{1,0:T(8,128)(2,1)} %bitcast.37), custom_call_target="tpu_custom_call" | custom-call | tf_op jit(solution)/shard_map/pallas_call | solution.py:54
  28.4 2.9 %collective-permute-start.4 = (bf16[2,128,512]{2,1,0:T(8,128)(2,1)}, bf16[2,128,512]{2,1,0:T(8,128)(2,1)S(1)}, u32[]{:S(2)}, u32[]{:S(2)}) collective-permute-start(bf16[2,128,512]{2,1,0:T(8,128)(2,1)} %get-tuple-element.53), channel_id=1, source_target_pairs={{0,64},{16,80},{32,96},{48,112},{64,0},{80,16},{96,32},{112,48},{1... | collective-permute-start | bytes 786440 | tf_op jit(solution)/shard_map/ppermute | solution.py:23
  31.3 10.4 %collective-permute-done.25.g2 = bf16[128,2048]{1,0:T(8,128)(2,1)S(1)} collective-permute-done((bf16[128,2048]{1,0:T(8,128)(2,1)S(1)}, bf16[128,2048]{1,0:T(8,128)(2,1)S(1)}, u32[]{:S(2)}, u32[]{:S(2)}) %collective-permute-start.25) | collective-permute-done | bytes 524320 | tf_op jit(solution)/shard_map/ppermute | solution.py:23
  41.8 10.2 %collective-permute-done.26.g3 = bf16[128,2048]{1,0:T(8,128)(2,1)S(1)} collective-permute-done((bf16[128,2048]{1,0:T(8,128)(2,1)S(1)}, bf16[128,2048]{1,0:T(8,128)(2,1)S(1)}, u32[]{:S(2)}, u32[]{:S(2)}) %collective-permute-start.26) | collective-permute-done | bytes 524320 | tf_op jit(solution)/shard_map/ppermute | solution.py:23
  54.5 5.1 %shard_map.123 = (bf16[512,512]{1,0:T(8,128)(2,1)}, bf16[512,512]{1,0:T(8,128)(2,1)}) custom-call(s32[2]{0:T(128)} %pad_add_fusion.place_ref, bf16[128,2048]{1,0:T(8,128)(2,1)} %bitcast.29, bf16[128,2048]{1,0:T(8,128)(2,1)} %copy-done.16, bf16[128,2048]{1,0:T(8,128)(2,1)} %copy-done.17, bf16[128,2048]{1,0:T(8,128)(2,1)} %copy-done.18, ...), custom_call_target="tpu_custom_call" | custom-call | tf_op jit(solution)/shard_map/pallas_call | solution.py:54
  65.6 7.1 %collective-permute-done.7.refs_9_ = bf16[2,128,512]{2,1,0:T(8,128)(2,1)S(1)} collective-permute-done((bf16[2,128,512]{2,1,0:T(8,128)(2,1)S(1)}, bf16[2,128,512]{2,1,0:T(8,128)(2,1)S(1)}, u32[]{:S(2)}, u32[]{:S(2)}) %collective-permute-start.7) | collective-permute-done | bytes 262176 | tf_op jit(solution)/shard_map/ppermute | solution.py:23
  72.7 5.6 %collective-permute-done.8.refs_10_ = bf16[2,128,512]{2,1,0:T(8,128)(2,1)S(1)} collective-permute-done((bf16[2,128,512]{2,1,0:T(8,128)(2,1)S(1)}, bf16[2,128,512]{2,1,0:T(8,128)(2,1)S(1)}, u32[]{:S(2)}, u32[]{:S(2)}) %collective-permute-start.8) | collective-permute-done | bytes 262176 | tf_op jit(solution)/shard_map/ppermute | solution.py:23
  78.3 4.2 %collective-permute-done.9.refs_11_ = bf16[2,128,512]{2,1,0:T(8,128)(2,1)S(1)} collective-permute-done((bf16[2,128,512]{2,1,0:T(8,128)(2,1)S(1)}, bf16[2,128,512]{2,1,0:T(8,128)(2,1)S(1)}, u32[]{:S(2)}, u32[]{:S(2)}) %collective-permute-start.9) | collective-permute-done | bytes 262176 | tf_op jit(solution)/shard_map/ppermute | solution.py:23
  83.4 9.6 %shard_map.120 = (f32[512,512]{1,0:T(8,128)}, bf16[512,512]{1,0:T(8,128)(2,1)}, bf16[512,512]{1,0:T(8,128)(2,1)}, bf16[512,512]{1,0:T(8,128)(2,1)}) custom-call(s32[2]{0:T(128)} %pad_add_fusion.place_ref, bf16[1,128,512]{2,1,0:T(8,128)(2,1)} %get-tuple-element.47.refs_0_, bf16[1,128,512]{2,1,0:T(8,128)(2,1)} %copy-done.22, bf16[1,128,512]{2,1,0:T(8,128)(2,1)} %copy-done.23, ...), custom_call_target="tpu_custom_call" | custom-call | tf_op jit(solution)/shard_map/pallas_call | solution.py:54
  94.7 2.5 %collective-permute-start.15 = (bf16[512,512]{1,0:T(8,128)(2,1)}, bf16[512,512]{1,0:T(8,128)(2,1)S(1)}, u32[]{:S(2)}, u32[]{:S(2)}) collective-permute-start(bf16[512,512]{1,0:T(8,128)(2,1)} %get-tuple-element.60), channel_id=1, source_target_pairs={{0,32},{16,48},{32,0},{48,16},{64,96},{80,112},{96,64},{112,80},{1... | collective-permute-start | bytes 1572872 | tf_op jit(solution)/shard_map/ppermute | solution.py:23
  97.2 2.6 %shard_map.121 = (bf16[1,128,512]{2,1,0:T(8,128)(2,1)}, bf16[1,128,512]{2,1,0:T(8,128)(2,1)}, bf16[1,128,512]{2,1,0:T(8,128)(2,1)}, bf16[1,128,512]{2,1,0:T(8,128)(2,1)}) custom-call(s32[2]{0:T(128)} %pad_add_fusion.place_ref, bf16[128,2048]{1,0:T(8,128)(2,1)} %bitcast.35), custom_call_target="tpu_custom_call" | custom-call | tf_op jit(solution)/shard_map/pallas_call | solution.py:54
  101.4 19.8 %collective-permute-done.14 = bf16[1,128,512]{2,1,0:T(8,128)(2,1)S(1)} collective-permute-done((bf16[1,128,512]{2,1,0:T(8,128)(2,1)}, bf16[1,128,512]{2,1,0:T(8,128)(2,1)S(1)}, u32[]{:S(2)}, u32[]{:S(2)}) %collective-permute-start.14) | collective-permute-done | bytes 131104 | tf_op jit(solution)/shard_map/ppermute | solution.py:23
  123.1 6.2 %collective-permute-done.13 = bf16[1,128,512]{2,1,0:T(8,128)(2,1)S(1)} collective-permute-done((bf16[1,128,512]{2,1,0:T(8,128)(2,1)}, bf16[1,128,512]{2,1,0:T(8,128)(2,1)S(1)}, u32[]{:S(2)}, u32[]{:S(2)}) %collective-permute-start.13) | collective-permute-done | bytes 131104 | tf_op jit(solution)/shard_map/ppermute | solution.py:23
  135.4 8.7 %collective-permute-done.28.c1.refs_13_ = bf16[512,512]{1,0:T(8,128)(2,1)S(1)} collective-permute-done((bf16[512,512]{1,0:T(8,128)(2,1)S(1)}, bf16[512,512]{1,0:T(8,128)(2,1)S(1)}, u32[]{:S(2)}, u32[]{:S(2)}) %collective-permute-start.28) | collective-permute-done | bytes 524320 | tf_op jit(solution)/shard_map/ppermute | solution.py:23
  144.1 8.7 %collective-permute-done.29.c2.refs_14_ = bf16[512,512]{1,0:T(8,128)(2,1)S(1)} collective-permute-done((bf16[512,512]{1,0:T(8,128)(2,1)S(1)}, bf16[512,512]{1,0:T(8,128)(2,1)S(1)}, u32[]{:S(2)}, u32[]{:S(2)}) %collective-permute-start.29) | collective-permute-done | bytes 524320 | tf_op jit(solution)/shard_map/ppermute | solution.py:23
  155.0 8.9 %shard_map.126 = (bf16[512,256]{1,0:T(8,128)(2,1)}, bf16[2,512,256]{2,1,0:T(8,128)(2,1)}, bf16[2,512,256]{2,1,0:T(8,128)(2,1)}) custom-call(s32[2]{0:T(128)} %pad_add_fusion.place_ref, bf16[1,128,512]{2,1,0:T(8,128)(2,1)} %get-tuple-element.47.refs_0_, bf16[1,128,512]{2,1,0:T(8,128)(2,1)} %copy-done.22, bf16[1,128,512]{2,1,0:T(8,128)(2,1)} %copy-done.23, ...), custom_call_target="tpu_custom_call" | custom-call | tf_op jit(solution)/shard_map/pallas_call | solution.py:54
  166.8 5.2 %shard_map.122 = (f32[128,2048]{1,0:T(8,128)}, bf16[128,2048]{1,0:T(8,128)(2,1)}, bf16[128,2048]{1,0:T(8,128)(2,1)}, bf16[128,2048]{1,0:T(8,128)(2,1)}) custom-call(s32[2]{0:T(128)} %pad_add_fusion.place_ref, bf16[512,512]{1,0:T(8,128)(2,1)} %copy-done.21, bf16[512,512]{1,0:T(8,128)(2,1)} %copy-done.20, bf16[256,2048]{1,0:T(8,128)(2,1)} %bitcast.26, ...), custom_call_target="tpu_custom_call" | custom-call | tf_op jit(solution)/shard_map/pallas_call | solution.py:54
  173.3 8.9 %shard_map.125 = (bf16[512,256]{1,0:T(8,128)(2,1)}, bf16[2,512,256]{2,1,0:T(8,128)(2,1)}, bf16[2,512,256]{2,1,0:T(8,128)(2,1)}) custom-call(s32[2]{0:T(128)} %pad_add_fusion.place_ref, bf16[1,128,512]{2,1,0:T(8,128)(2,1)} %get-tuple-element.47.refs_0_, bf16[1,128,512]{2,1,0:T(8,128)(2,1)} %copy-done.22, bf16[1,128,512]{2,1,0:T(8,128)(2,1)} %copy-done.23, ...), custom_call_target="tpu_custom_call" | custom-call | tf_op jit(solution)/shard_map/pallas_call | solution.py:54
  186.5 4.9 %shard_map.130 = (f32[256,2048]{1,0:T(8,128)}, bf16[256,2048]{1,0:T(8,128)(2,1)}) custom-call(s32[2]{0:T(128)} %pad_add_fusion.place_ref, bf16[512,512]{1,0:T(8,128)(2,1)} %copy-done.21, bf16[128,2048]{1,0:T(8,128)(2,1)} %bitcast.30, bf16[128,2048]{1,0:T(8,128)(2,1)} %copy-done.16, bf16[128,2048]{1,0:T(8,128)(2,1)} %copy-done.17, bf16[128,2048]{1,0:T(8,128)(2,1)} %copy-done.18), custom_call_target="tpu_custom_call" | custom-call | tf_op jit(solution)/shard_map/pallas_call | solution.py:54
  193.6 2.7 %shard_map.127 = (bf16[2,128,256]{2,1,0:T(8,128)(2,1)}, bf16[2,128,256]{2,1,0:T(8,128)(2,1)}, bf16[2,128,256]{2,1,0:T(8,128)(2,1)}, bf16[2,128,256]{2,1,0:T(8,128)(2,1)}) custom-call(s32[2]{0:T(128)} %pad_add_fusion.place_ref, bf16[2,512,256]{2,1,0:T(8,128)(2,1)} %get-tuple-element.69.a, bf16[2,512,256]{2,1,0:T(8,128)(2,1)} %copy-done.29), custom_call_target="tpu_custom_call" | custom-call | tf_op jit(solution)/shard_map/pallas_call | solution.py:54
  196.3 2.8 %collective-permute-start.33 = (bf16[2,128,256]{2,1,0:T(8,128)(2,1)}, bf16[2,128,256]{2,1,0:T(8,128)(2,1)S(1)}, u32[]{:S(2)}, u32[]{:S(2)}) collective-permute-start(bf16[2,128,256]{2,1,0:T(8,128)(2,1)} %get-tuple-element.73), channel_id=1, source_target_pairs={{0,64},{16,80},{32,96},{48,112},{64,0},{80,16},{96,32},{112,48},{1... | collective-permute-start | bytes 393224 | tf_op jit(solution)/shard_map/ppermute | solution.py:23
  199.1 2.6 %shard_map.124 = bf16[128,2048]{1,0:T(8,128)(2,1)} custom-call(s32[2]{0:T(128)} %pad_add_fusion.place_ref, bf16[512,512]{1,0:T(8,128)(2,1)} %copy-done, bf16[512,512]{1,0:T(8,128)(2,1)} %copy-done.1, bf16[512,512]{1,0:T(8,128)(2,1)} %copy-done.2, bf16[512,512]{1,0:T(8,128)(2,1)} %copy-done.3), custom_call_target="tpu_custom_call" | custom-call | tf_op jit(solution)/shard_map/pallas_call | solution.py:54
  201.7 3.0 %shard_map.128 = (bf16[4,128,256]{2,1,0:T(8,128)(2,1)}, bf16[4,128,256]{2,1,0:T(8,128)(2,1)}, bf16[4,128,256]{2,1,0:T(8,128)(2,1)}, bf16[4,128,256]{2,1,0:T(8,128)(2,1)}) custom-call(s32[2]{0:T(128)} %pad_add_fusion.place_ref, bf16[2,512,256]{2,1,0:T(8,128)(2,1)} %get-tuple-element.75.a, bf16[2,512,256]{2,1,0:T(8,128)(2,1)} %copy-done.28, ...), custom_call_target="tpu_custom_call" | custom-call | tf_op jit(solution)/shard_map/pallas_call | solution.py:54
  206.8 3.7 %collective-permute-done.21 = bf16[128,2048]{1,0:T(8,128)(2,1)S(1)} collective-permute-done((bf16[128,2048]{1,0:T(8,128)(2,1)S(1)}, bf16[128,2048]{1,0:T(8,128)(2,1)S(1)}, u32[]{:S(2)}, u32[]{:S(2)}) %collective-permute-start.21) | collective-permute-done | bytes 524320 | tf_op jit(solution)/shard_map/ppermute | solution.py:23
  210.5 2.8 %collective-permute-done.32.refs_1_ = bf16[2,128,256]{2,1,0:T(8,128)(2,1)S(1)} collective-permute-done((bf16[2,128,256]{2,1,0:T(8,128)(2,1)}, bf16[2,128,256]{2,1,0:T(8,128)(2,1)S(1)}, u32[]{:S(2)}, u32[]{:S(2)}) %collective-permute-start.32) | collective-permute-done | bytes 131104 | tf_op jit(solution)/shard_map/ppermute | solution.py:23
  214.5 3.1 %collective-permute-done.33.refs_2_ = bf16[2,128,256]{2,1,0:T(8,128)(2,1)S(1)} collective-permute-done((bf16[2,128,256]{2,1,0:T(8,128)(2,1)}, bf16[2,128,256]{2,1,0:T(8,128)(2,1)S(1)}, u32[]{:S(2)}, u32[]{:S(2)}) %collective-permute-start.33) | collective-permute-done | bytes 131104 | tf_op jit(solution)/shard_map/ppermute | solution.py:23
  220.4 2.7 %collective-permute-done.37.refs_6_ = bf16[4,128,256]{2,1,0:T(8,128)(2,1)S(1)} collective-permute-done((bf16[4,128,256]{2,1,0:T(8,128)(2,1)}, bf16[4,128,256]{2,1,0:T(8,128)(2,1)S(1)}, u32[]{:S(2)}, u32[]{:S(2)}) %collective-permute-start.37) | collective-permute-done | bytes 262176 | tf_op jit(solution)/shard_map/ppermute | solution.py:23
  223.1 2.7 %collective-permute-done.38.refs_7_ = bf16[4,128,256]{2,1,0:T(8,128)(2,1)S(1)} collective-permute-done((bf16[4,128,256]{2,1,0:T(8,128)(2,1)}, bf16[4,128,256]{2,1,0:T(8,128)(2,1)S(1)}, u32[]{:S(2)}, u32[]{:S(2)}) %collective-permute-start.38) | collective-permute-done | bytes 262176 | tf_op jit(solution)/shard_map/ppermute | solution.py:23
  226.6 3.4 %shard_map.129 = (bf16[128,2048]{1,0:T(8,128)(2,1)}, bf16[128,2048]{1,0:T(8,128)(2,1)}, bf16[128,2048]{1,0:T(8,128)(2,1)}) custom-call(s32[2]{0:T(128)} %pad_add_fusion.place_ref, bf16[2,128,256]{2,1,0:T(8,128)(2,1)} %get-tuple-element.71.refs_0_, bf16[2,128,256]{2,1,0:T(8,128)(2,1)} %copy-done.33, bf16[2,128,256]{2,1,0:T(8,128)(2,1)} %copy-done.34, ...), custom_call_target="tpu_custom_call" | custom-call | tf_op jit(solution)/shard_map/pallas_call | solution.py:54
  (146 shorter events, 57.1 us)
Async XLA Ops:
  1.8 18.9 %collective-permute-start.19 = (bf16[128,2048]{1,0:T(8,128)(2,1)S(1)}, bf16[128,2048]{1,0:T(8,128)(2,1)S(1)}, u32[]{:S(2)}, u32[]{:S(2)}) collective-permute-start(bf16[128,2048]{1,0:T(8,128)(2,1)S(1)} %dynamic-slice_bitcast_fusion), channel_id=1, source_target_pairs={{0,17},{1,16},{2,19},{3,18},{4,21},{5,20},{6,23},{7,22},{8,25},{9,... | collective-permute-start | bytes 1572872 | tf_op jit(solution)/shard_map/ppermute | solution.py:35
  12.4 14.4 %collective-permute-start.10 = (bf16[128,2048]{1,0:T(8,128)(2,1)S(1)}, bf16[128,2048]{1,0:T(8,128)(2,1)S(1)}, u32[]{:S(2)}, u32[]{:S(2)}) collective-permute-start(bf16[128,2048]{1,0:T(8,128)(2,1)S(1)} %dynamic-slice_bitcast_fusion.1), channel_id=1, source_target_pairs={{0,17},{1,16},{2,19},{3,18},{4,21},{5,20},{6,23},{7,22},{8,25},{9,... | collective-permute-start | bytes 1572872 | tf_op jit(solution)/shard_map/ppermute | solution.py:35
  13.0 15.4 %collective-permute-start.24 = (bf16[128,2048]{1,0:T(8,128)(2,1)S(1)}, bf16[128,2048]{1,0:T(8,128)(2,1)S(1)}, u32[]{:S(2)}, u32[]{:S(2)}) collective-permute-start(bf16[128,2048]{1,0:T(8,128)(2,1)S(1)} %bitcast.31), channel_id=1, source_target_pairs={{0,32},{16,48},{32,0},{48,16},{64,96},{80,112},{96,64},{112,80},{1... | collective-permute-start | bytes 1572872 | tf_op jit(solution)/shard_map/ppermute | solution.py:23
  17.5 24.2 %collective-permute-start.25 = (bf16[128,2048]{1,0:T(8,128)(2,1)S(1)}, bf16[128,2048]{1,0:T(8,128)(2,1)S(1)}, u32[]{:S(2)}, u32[]{:S(2)}) collective-permute-start(bf16[128,2048]{1,0:T(8,128)(2,1)S(1)} %bitcast.32), channel_id=1, source_target_pairs={{0,64},{16,80},{32,96},{48,112},{64,0},{80,16},{96,32},{112,48},{1... | collective-permute-start | bytes 1572872 | tf_op jit(solution)/shard_map/ppermute | solution.py:23
  19.1 32.9 %collective-permute-start.26 = (bf16[128,2048]{1,0:T(8,128)(2,1)S(1)}, bf16[128,2048]{1,0:T(8,128)(2,1)S(1)}, u32[]{:S(2)}, u32[]{:S(2)}) collective-permute-start(bf16[128,2048]{1,0:T(8,128)(2,1)S(1)} %bitcast.33), channel_id=1, source_target_pairs={{0,96},{16,112},{32,64},{48,80},{64,32},{80,48},{96,0},{112,16},{1... | collective-permute-start | bytes 1572872 | tf_op jit(solution)/shard_map/ppermute | solution.py:23
  20.7 31.3 %collective-permute-start.20 = (bf16[128,2048]{1,0:T(8,128)(2,1)S(1)}, bf16[128,2048]{1,0:T(8,128)(2,1)S(1)}, u32[]{:S(2)}, u32[]{:S(2)}) collective-permute-start(bf16[128,2048]{1,0:T(8,128)(2,1)S(1)} %collective-permute-done.19.mine), channel_id=1, source_target_pairs={{0,1},{1,0},{2,3},{3,2},{4,5},{5,4},{6,7},{7,6},{8,9},{9,8},{10,11... | collective-permute-start | bytes 1572872 | tf_op jit(solution)/shard_map/ppermute | solution.py:35
  26.8 32.8 %collective-permute-start.3 = (bf16[2,128,512]{2,1,0:T(8,128)(2,1)}, bf16[2,128,512]{2,1,0:T(8,128)(2,1)S(1)}, u32[]{:S(2)}, u32[]{:S(2)}) collective-permute-start(bf16[2,128,512]{2,1,0:T(8,128)(2,1)} %get-tuple-element.52), channel_id=1, source_target_pairs={{0,32},{16,48},{32,0},{48,16},{64,96},{80,112},{96,64},{112,80},{1... | collective-permute-start | bytes 786440 | tf_op jit(solution)/shard_map/ppermute | solution.py:23
  28.4 31.4 %collective-permute-start.4 = (bf16[2,128,512]{2,1,0:T(8,128)(2,1)}, bf16[2,128,512]{2,1,0:T(8,128)(2,1)S(1)}, u32[]{:S(2)}, u32[]{:S(2)}) collective-permute-start(bf16[2,128,512]{2,1,0:T(8,128)(2,1)} %get-tuple-element.53), channel_id=1, source_target_pairs={{0,64},{16,80},{32,96},{48,112},{64,0},{80,16},{96,32},{112,48},{1... | collective-permute-start | bytes 786440 | tf_op jit(solution)/shard_map/ppermute | solution.py:23
  41.7 20.4 %collective-permute-start.5 = (bf16[2,128,512]{2,1,0:T(8,128)(2,1)}, bf16[2,128,512]{2,1,0:T(8,128)(2,1)S(1)}, u32[]{:S(2)}, u32[]{:S(2)}) collective-permute-start(bf16[2,128,512]{2,1,0:T(8,128)(2,1)} %get-tuple-element.54), channel_id=1, source_target_pairs={{0,96},{16,112},{32,64},{48,80},{64,32},{80,48},{96,0},{112,16},{1... | collective-permute-start | bytes 786440 | tf_op jit(solution)/shard_map/ppermute | solution.py:23
  52.0 11.4 %collective-permute-start.6 = (bf16[2,128,512]{2,1,0:T(8,128)(2,1)}, bf16[2,128,512]{2,1,0:T(8,128)(2,1)S(1)}, u32[]{:S(2)}, u32[]{:S(2)}) collective-permute-start(bf16[2,128,512]{2,1,0:T(8,128)(2,1)} %get-tuple-element.51.refs_4_), channel_id=1, source_target_pairs={{0,16},{16,0},{32,48},{48,32},{64,80},{80,64},{96,112},{112,96},{1... | collective-permute-start | bytes 786440 | tf_op jit(solution)/shard_map/ppermute | solution.py:23
  52.0 30.5 %collective-permute-start.11 = (bf16[128,2048]{1,0:T(8,128)(2,1)S(1)}, bf16[128,2048]{1,0:T(8,128)(2,1)S(1)}, u32[]{:S(2)}, u32[]{:S(2)}) collective-permute-start(bf16[128,2048]{1,0:T(8,128)(2,1)S(1)} %collective-permute-done.10.refs_13_.refs_16_), channel_id=1, source_target_pairs={{0,1},{1,0},{2,3},{3,2},{4,5},{5,4},{6,7},{7,6},{8,9},{9,8},{10,11... | collective-permute-start | bytes 1572872 | tf_op jit(solution)/shard_map/ppermute | solution.py:35
  59.6 61.5 %collective-permute-start.27 = (bf16[512,512]{1,0:T(8,128)(2,1)}, bf16[512,512]{1,0:T(8,128)(2,1)S(1)}, u32[]{:S(2)}, u32[]{:S(2)}) collective-permute-start(bf16[512,512]{1,0:T(8,128)(2,1)} %get-tuple-element.68), channel_id=1, source_target_pairs={{0,128},{128,0},{1,129},{129,1},{2,130},{130,2},{3,131},{131,3},{4... | collective-permute-start | bytes 1572872 | tf_op jit(solution)/shard_map/ppermute | solution.py:27
  59.8 12.9 %collective-permute-start.7 = (bf16[2,128,512]{2,1,0:T(8,128)(2,1)S(1)}, bf16[2,128,512]{2,1,0:T(8,128)(2,1)S(1)}, u32[]{:S(2)}, u32[]{:S(2)}) collective-permute-start(bf16[2,128,512]{2,1,0:T(8,128)(2,1)S(1)} %collective-permute-done.3.refs_5_), channel_id=1, source_target_pairs={{0,16},{16,0},{32,48},{48,32},{64,80},{80,64},{96,112},{112,96},{1... | collective-permute-start | bytes 786440 | tf_op jit(solution)/shard_map/ppermute | solution.py:23
  62.1 16.2 %collective-permute-start.8 = (bf16[2,128,512]{2,1,0:T(8,128)(2,1)S(1)}, bf16[2,128,512]{2,1,0:T(8,128)(2,1)S(1)}, u32[]{:S(2)}, u32[]{:S(2)}) collective-permute-start(bf16[2,128,512]{2,1,0:T(8,128)(2,1)S(1)} %collective-permute-done.4.refs_6_), channel_id=1, source_target_pairs={{0,16},{16,0},{32,48},{48,32},{64,80},{80,64},{96,112},{112,96},{1... | collective-permute-start | bytes 786440 | tf_op jit(solution)/shard_map/ppermute | solution.py:23
  63.4 19.2 %collective-permute-start.9 = (bf16[2,128,512]{2,1,0:T(8,128)(2,1)S(1)}, bf16[2,128,512]{2,1,0:T(8,128)(2,1)S(1)}, u32[]{:S(2)}, u32[]{:S(2)}) collective-permute-start(bf16[2,128,512]{2,1,0:T(8,128)(2,1)S(1)} %collective-permute-done.5.refs_7_), channel_id=1, source_target_pairs={{0,16},{16,0},{32,48},{48,32},{64,80},{80,64},{96,112},{112,96},{1... | collective-permute-start | bytes 786440 | tf_op jit(solution)/shard_map/ppermute | solution.py:23
  93.1 38.6 %collective-permute-start.17 = (bf16[512,512]{1,0:T(8,128)(2,1)}, bf16[512,512]{1,0:T(8,128)(2,1)S(1)}, u32[]{:S(2)}, u32[]{:S(2)}) collective-permute-start(bf16[512,512]{1,0:T(8,128)(2,1)} %get-tuple-element.62), channel_id=1, source_target_pairs={{0,96},{16,112},{32,64},{48,80},{64,32},{80,48},{96,0},{112,16},{1... | collective-permute-start | bytes 1572872 | tf_op jit(solution)/shard_map/ppermute | solution.py:23
  94.7 39.3 %collective-permute-start.16 = (bf16[512,512]{1,0:T(8,128)(2,1)}, bf16[512,512]{1,0:T(8,128)(2,1)S(1)}, u32[]{:S(2)}, u32[]{:S(2)}) collective-permute-start(bf16[512,512]{1,0:T(8,128)(2,1)} %get-tuple-element.61), channel_id=1, source_target_pairs={{0,64},{16,80},{32,96},{48,112},{64,0},{80,16},{96,32},{112,48},{1... | collective-permute-start | bytes 1572872 | tf_op jit(solution)/shard_map/ppermute | solution.py:23
  94.7 39.3 %collective-permute-start.15 = (bf16[512,512]{1,0:T(8,128)(2,1)}, bf16[512,512]{1,0:T(8,128)(2,1)S(1)}, u32[]{:S(2)}, u32[]{:S(2)}) collective-permute-start(bf16[512,512]{1,0:T(8,128)(2,1)} %get-tuple-element.60), channel_id=1, source_target_pairs={{0,32},{16,48},{32,0},{48,16},{64,96},{80,112},{96,64},{112,80},{1... | collective-permute-start | bytes 1572872 | tf_op jit(solution)/shard_map/ppermute | solution.py:23
  99.8 21.3 %collective-permute-start.14 = (bf16[1,128,512]{2,1,0:T(8,128)(2,1)}, bf16[1,128,512]{2,1,0:T(8,128)(2,1)S(1)}, u32[]{:S(2)}, u32[]{:S(2)}) collective-permute-start(bf16[1,128,512]{2,1,0:T(8,128)(2,1)} %get-tuple-element.59), channel_id=1, source_target_pairs={{0,96},{16,112},{32,64},{48,80},{64,32},{80,48},{96,0},{112,16},{1... | collective-permute-start | bytes 393224 | tf_op jit(solution)/shard_map/ppermute | solution.py:23
  129.3 14.8 %collective-permute-start.28 = (bf16[512,512]{1,0:T(8,128)(2,1)S(1)}, bf16[512,512]{1,0:T(8,128)(2,1)S(1)}, u32[]{:S(2)}, u32[]{:S(2)}) collective-permute-start(bf16[512,512]{1,0:T(8,128)(2,1)S(1)} %add_convert_fusion.c0.refs_12_), channel_id=1, source_target_pairs={{0,32},{16,48},{32,0},{48,16},{64,96},{80,112},{96,64},{112,80},{1... | collective-permute-start | bytes 1572872 | tf_op jit(solution)/shard_map/ppermute | solution.py:23
  129.3 23.5 %collective-permute-start.29 = (bf16[512,512]{1,0:T(8,128)(2,1)S(1)}, bf16[512,512]{1,0:T(8,128)(2,1)S(1)}, u32[]{:S(2)}, u32[]{:S(2)}) collective-permute-start(bf16[512,512]{1,0:T(8,128)(2,1)S(1)} %add_convert_fusion.c0.refs_12_), channel_id=1, source_target_pairs={{0,64},{16,80},{32,96},{48,112},{64,0},{80,16},{96,32},{112,48},{1... | collective-permute-start | bytes 1572872 | tf_op jit(solution)/shard_map/ppermute | solution.py:23
  131.7 22.5 %collective-permute-start.30 = (bf16[512,512]{1,0:T(8,128)(2,1)S(1)}, bf16[512,512]{1,0:T(8,128)(2,1)S(1)}, u32[]{:S(2)}, u32[]{:S(2)}) collective-permute-start(bf16[512,512]{1,0:T(8,128)(2,1)S(1)} %add_convert_fusion.c0.refs_12_), channel_id=1, source_target_pairs={{0,96},{16,112},{32,64},{48,80},{64,32},{80,48},{96,0},{112,16},{1... | collective-permute-start | bytes 1572872 | tf_op jit(solution)/shard_map/ppermute | solution.py:23
  135.3 30.7 %collective-permute-start.18 = (bf16[512,512]{1,0:T(8,128)(2,1)S(1)}, bf16[512,512]{1,0:T(8,128)(2,1)S(1)}, u32[]{:S(2)}, u32[]{:S(2)}) collective-permute-start(bf16[512,512]{1,0:T(8,128)(2,1)S(1)} %add_convert_fusion.2.own_hid), channel_id=1, source_target_pairs={{0,128},{128,0},{1,129},{129,1},{2,130},{130,2},{3,131},{131,3},{4... | collective-permute-start | bytes 1572872 | tf_op jit(solution)/shard_map/ppermute | solution.py:27
  163.9 27.5 %collective-permute-start.31 = (bf16[2,512,256]{2,1,0:T(8,128)(2,1)}, bf16[2,512,256]{2,1,0:T(8,128)(2,1)S(1)}, u32[]{:S(2)}, u32[]{:S(2)}) collective-permute-start(bf16[2,512,256]{2,1,0:T(8,128)(2,1)} %get-tuple-element.70), channel_id=1, source_target_pairs={{0,16},{16,0},{32,48},{48,32},{64,80},{80,64},{96,112},{112,96},{1... | collective-permute-start | bytes 1572872 | tf_op jit(solution)/shard_map/ppermute | solution.py:23
  172.0 24.3 %collective-permute-start.23 = (bf16[128,2048]{1,0:T(8,128)(2,1)}, bf16[128,2048]{1,0:T(8,128)(2,1)S(1)}, u32[]{:S(2)}, u32[]{:S(2)}) collective-permute-start(bf16[128,2048]{1,0:T(8,128)(2,1)} %get-tuple-element.66), channel_id=1, source_target_pairs={{0,96},{16,112},{32,64},{48,80},{64,32},{80,48},{96,0},{112,16},{1... | collective-permute-start | bytes 1572872 | tf_op jit(solution)/shard_map/ppermute | solution.py:23
  182.2 14.1 %collective-permute-start.35 = (bf16[2,512,256]{2,1,0:T(8,128)(2,1)}, bf16[2,512,256]{2,1,0:T(8,128)(2,1)S(1)}, u32[]{:S(2)}, u32[]{:S(2)}) collective-permute-start(bf16[2,512,256]{2,1,0:T(8,128)(2,1)} %get-tuple-element.76), channel_id=1, source_target_pairs={{0,16},{16,0},{32,48},{48,32},{64,80},{80,64},{96,112},{112,96},{1... | collective-permute-start | bytes 1572872 | tf_op jit(solution)/shard_map/ppermute | solution.py:23
  184.5 20.3 %collective-permute-start.22 = (bf16[128,2048]{1,0:T(8,128)(2,1)S(1)}, bf16[128,2048]{1,0:T(8,128)(2,1)S(1)}, u32[]{:S(2)}, u32[]{:S(2)}) collective-permute-start(bf16[128,2048]{1,0:T(8,128)(2,1)S(1)} %copy-done.37), channel_id=1, source_target_pairs={{0,64},{16,80},{32,96},{48,112},{64,0},{80,16},{96,32},{112,48},{1... | collective-permute-start | bytes 1572872 | tf_op jit(solution)/shard_map/ppermute | solution.py:23
  184.8 25.7 %collective-permute-start.21 = (bf16[128,2048]{1,0:T(8,128)(2,1)S(1)}, bf16[128,2048]{1,0:T(8,128)(2,1)S(1)}, u32[]{:S(2)}, u32[]{:S(2)}) collective-permute-start(bf16[128,2048]{1,0:T(8,128)(2,1)S(1)} %copy-done.36), channel_id=1, source_target_pairs={{0,32},{16,48},{32,0},{48,16},{64,96},{80,112},{96,64},{112,80},{1... | collective-permute-start | bytes 1572872 | tf_op jit(solution)/shard_map/ppermute | solution.py:23
  191.4 38.5 %collective-permute-start.39 = (bf16[256,2048]{1,0:T(8,128)(2,1)}, bf16[256,2048]{1,0:T(8,128)(2,1)S(1)}, u32[]{:S(2)}, u32[]{:S(2)}) collective-permute-start(bf16[256,2048]{1,0:T(8,128)(2,1)} %get-tuple-element.87), channel_id=1, source_target_pairs={{0,16},{16,0},{32,48},{48,32},{64,80},{80,64},{96,112},{112,96},{1... | collective-permute-start | bytes 3145736 | tf_op jit(solution)/shard_map/ppermute | solution.py:23
  196.3 17.0 %collective-permute-start.32 = (bf16[2,128,256]{2,1,0:T(8,128)(2,1)}, bf16[2,128,256]{2,1,0:T(8,128)(2,1)S(1)}, u32[]{:S(2)}, u32[]{:S(2)}) collective-permute-start(bf16[2,128,256]{2,1,0:T(8,128)(2,1)} %get-tuple-element.72), channel_id=1, source_target_pairs={{0,32},{16,48},{32,0},{48,16},{64,96},{80,112},{96,64},{112,80},{1... | collective-permute-start | bytes 393224 | tf_op jit(solution)/shard_map/ppermute | solution.py:23
  196.3 21.2 %collective-permute-start.33 = (bf16[2,128,256]{2,1,0:T(8,128)(2,1)}, bf16[2,128,256]{2,1,0:T(8,128)(2,1)S(1)}, u32[]{:S(2)}, u32[]{:S(2)}) collective-permute-start(bf16[2,128,256]{2,1,0:T(8,128)(2,1)} %get-tuple-element.73), channel_id=1, source_target_pairs={{0,64},{16,80},{32,96},{48,112},{64,0},{80,16},{96,32},{112,48},{1... | collective-permute-start | bytes 393224 | tf_op jit(solution)/shard_map/ppermute | solution.py:23
  204.8 15.2 %collective-permute-start.34 = (bf16[2,128,256]{2,1,0:T(8,128)(2,1)S(1)}, bf16[2,128,256]{2,1,0:T(8,128)(2,1)S(1)}, u32[]{:S(2)}, u32[]{:S(2)}) collective-permute-start(bf16[2,128,256]{2,1,0:T(8,128)(2,1)S(1)} %copy-done.38), channel_id=1, source_target_pairs={{0,96},{16,112},{32,64},{48,80},{64,32},{80,48},{96,0},{112,16},{1... | collective-permute-start | bytes 393224 | tf_op jit(solution)/shard_map/ppermute | solution.py:23
  (47 other events, 687.6 us)

commit v2 on v1

--- a/solution.py
+++ b/solution.py
@@ -289,20 +289,28 @@
     )
 
 
-def gradient_columns(place, low, high):
+def query_columns(place, high):
+    def body(place_ref, h0, h1, h2, h3, out):
+        for r, ref in enumerate((h0, h1, h2, h3)):
+            out[:, chunk(place_ref, 2 * r)] = ref[2]
+            out[:, chunk(place_ref, 2 * r + 1)] = ref[3]
+
+    shape = (TOK, 8 * CHUNK)
+    return call(body, [], [shape], [sds(shape)], place, high)[0]
+
+
+def key_columns(place, low, high):
     def body(place_ref, *refs):
-        lows, highs, (q_out, k_out, v_out) = refs[:4], refs[4:8], refs[8:]
+        lows, highs, outs = refs[:4], refs[4:8], refs[8:]
         for r in range(4):
-            even, odd = chunk(place_ref, 2 * r), chunk(place_ref, 2 * r + 1)
-            q_out[:, even] = highs[r][2]
-            q_out[:, odd] = highs[r][3]
-            k_out[:, even] = lows[r][0]
-            k_out[:, odd] = highs[r][0]
-            v_out[:, even] = lows[r][1]
-            v_out[:, odd] = highs[r][1]
-
+            for t, out in enumerate(outs):
+                out[:, chunk(place_ref, 2 * r)] = lows[r][t]
+                out[:, chunk(place_ref, 2 * r + 1)] = highs[r][t]
+
+    pair = pl.BlockSpec((2, TOK, CHUNK), lambda i, place: (0, 0, 0))
     shape = (TOK, 8 * CHUNK)
-    return call(body, [], [shape] * 3, [sds(shape)] * 3, place, (*low, *high))
+    args = (*low, *high)
+    return call(body, [pair] * 8, [shape] * 2, [sds(shape)] * 2, place, args)
 
 
 def grad_hidden_columns(place, chunks):
@@ -329,7 +337,8 @@
     pairs = relative_columns(place, (key_vecs[0], value_vecs[0]))
     pairs = exchange(pairs)
     others = [seq_shift(pairs[r], 1) for r in range(4)]
-    couple_half = rep_shift(half_rows(couple_proj[0], odd_rep), 1)
+    couple_sent = half_rows(couple_proj[0], odd_rep)
+    couple_half = rep_shift(couple_sent, 1)
     proj_half = rep_shift(half_rows(out_proj[0], odd_rep), 1)
     grads = exchange([grad_mixed[0]] * 4)
     items = exchange(relative_columns(place, (queries[0],)))
@@ -367,10 +376,12 @@
     mixed = mixed_parts[0]
     for part in mixed_parts[1:]:
         mixed = mixed + part.astype(F32)
+    mixed = mixed.astype(BF16)[None]
     grad_cpl = couple_own + couple_got.astype(F32)
-    grad_q, grad_k, grad_v = gradient_columns(place, low, high)
+    grad_q = query_columns(place, high)
+    grad_k, grad_v = key_columns(place, low, high)
     return (
-        mixed.astype(BF16)[None],
+        mixed,
         grad_hid[None],
         grad_q[None],
         grad_k[None],

time: 232 us -> 234 us (level)
  waiting for transfers between devices: 103 us -> 99.9 us
  Pallas kernels: 62.5 us -> 65 us
    ppermute x34, waiting for transfers between devices: 102 us -> 98.6 us  [seq_shift(): return lax.ppermute(value, 'seq', [(i, i ^ mask) for i in range(size)])]
    pallas_call x13 -> x14, Pallas kernels: 62.5 us -> 65 us  [call(): pl.pallas_call(body, out_shape=out_shapes, grid_spec=pltpu.PrefetchScalar...]
  transfers between devices with their start and end apart: 40 -> 40, of which waited for: 18 -> 15; matrix products, arithmetic and copies ran while one was open for 2% -> 2% of each run, Pallas kernels for 27% -> 28%
where the time goes in v2:
time: 234 us; the launch traced here: 233 us
  waiting for transfers between devices  99.9 us (43%)
  Pallas kernels  65 us (28%)
  starting transfers between devices  56.5 us (24%)
  local copies, waits for them, and re-layouts  6.2 us (3%)
  other arithmetic  4.8 us (2%)
    ppermute x34, waiting for transfers between devices, seq_shift(): return lax.ppermute(value, 'seq', [(i, i ^ mask) for i in range(size)])  98.6 us
    pallas_call x14, Pallas kernels, call(): pl.pallas_call(body, out_shape=out_shapes, grid_spec=pltpu.PrefetchScalar...  65 us
    ppermute x34, starting transfers between devices, seq_shift(): return lax.ppermute(value, 'seq', [(i, i ^ mask) for i in range(size)])  49.7 us
    ppermute x4, starting transfers between devices, rep_shift(): return lax.ppermute(value, ('seq', 'rep'), pairs)  6.55 us
  transfers between devices with their start and end apart: 40, of which 15 were waited for; matrix products, arithmetic and copies ran while one was open for 2% of the time, Pallas kernels for 28%

profile of v2, /device:TPU:2, one launch (start us, length us, event | category | flops | bytes accessed | tf_op | source)
XLA Modules:
  0.0 233.3 jit_solution(1770940340216429370)
XLA Ops:
  4.0 2.6 %shard_map.118 = (bf16[1,128,512]{2,1,0:T(8,128)(2,1)}, bf16[1,128,512]{2,1,0:T(8,128)(2,1)}, bf16[1,128,512]{2,1,0:T(8,128)(2,1)}, bf16[1,128,512]{2,1,0:T(8,128)(2,1)}) custom-call(s32[2]{0:T(128)} %pad_add_fusion.place_ref, bf16[128,2048]{1,0:T(8,128)(2,1)} %bitcast.34), custom_call_target="tpu_custom_call" | custom-call | tf_op jit(solution)/shard_map/pallas_call | solution.py:54
  8.2 2.9 %collective-permute-start.1 = (bf16[1,128,512]{2,1,0:T(8,128)(2,1)}, bf16[1,128,512]{2,1,0:T(8,128)(2,1)S(1)}, u32[]{:S(2)}, u32[]{:S(2)}) collective-permute-start(bf16[1,128,512]{2,1,0:T(8,128)(2,1)} %get-tuple-element.48), channel_id=1, source_target_pairs={{0,64},{16,80},{32,96},{48,112},{64,0},{80,16},{96,32},{112,48},{1... | collective-permute-start | bytes 393224 | tf_op jit(solution)/shard_map/ppermute | solution.py:23
  13.5 3.9 %collective-permute-done.1.refs_2_ = bf16[1,128,512]{2,1,0:T(8,128)(2,1)S(1)} collective-permute-done((bf16[1,128,512]{2,1,0:T(8,128)(2,1)}, bf16[1,128,512]{2,1,0:T(8,128)(2,1)S(1)}, u32[]{:S(2)}, u32[]{:S(2)}) %collective-permute-start.1) | collective-permute-done | bytes 131104 | tf_op jit(solution)/shard_map/ppermute | solution.py:23
  22.6 3.0 %shard_map.119 = (bf16[2,128,512]{2,1,0:T(8,128)(2,1)}, bf16[2,128,512]{2,1,0:T(8,128)(2,1)}, bf16[2,128,512]{2,1,0:T(8,128)(2,1)}, bf16[2,128,512]{2,1,0:T(8,128)(2,1)}) custom-call(s32[2]{0:T(128)} %pad_add_fusion.place_ref, bf16[128,2048]{1,0:T(8,128)(2,1)} %bitcast.37, bf16[128,2048]{1,0:T(8,128)(2,1)} %bitcast.38), custom_call_target="tpu_custom_call" | custom-call | tf_op jit(solution)/shard_map/pallas_call | solution.py:54
  28.4 2.9 %collective-permute-start.4 = (bf16[2,128,512]{2,1,0:T(8,128)(2,1)}, bf16[2,128,512]{2,1,0:T(8,128)(2,1)S(1)}, u32[]{:S(2)}, u32[]{:S(2)}) collective-permute-start(bf16[2,128,512]{2,1,0:T(8,128)(2,1)} %get-tuple-element.52), channel_id=1, source_target_pairs={{0,64},{16,80},{32,96},{48,112},{64,0},{80,16},{96,32},{112,48},{1... | collective-permute-start | bytes 786440 | tf_op jit(solution)/shard_map/ppermute | solution.py:23
  31.3 10.4 %collective-permute-done.25.g2 = bf16[128,2048]{1,0:T(8,128)(2,1)S(1)} collective-permute-done((bf16[128,2048]{1,0:T(8,128)(2,1)S(1)}, bf16[128,2048]{1,0:T(8,128)(2,1)S(1)}, u32[]{:S(2)}, u32[]{:S(2)}) %collective-permute-start.25) | collective-permute-done | bytes 524320 | tf_op jit(solution)/shard_map/ppermute | solution.py:23
  41.8 10.2 %collective-permute-done.26.g3 = bf16[128,2048]{1,0:T(8,128)(2,1)S(1)} collective-permute-done((bf16[128,2048]{1,0:T(8,128)(2,1)S(1)}, bf16[128,2048]{1,0:T(8,128)(2,1)S(1)}, u32[]{:S(2)}, u32[]{:S(2)}) %collective-permute-start.26) | collective-permute-done | bytes 524320 | tf_op jit(solution)/shard_map/ppermute | solution.py:23
  54.5 5.1 %shard_map.123 = (bf16[512,512]{1,0:T(8,128)(2,1)}, bf16[512,512]{1,0:T(8,128)(2,1)}) custom-call(s32[2]{0:T(128)} %pad_add_fusion.place_ref, bf16[128,2048]{1,0:T(8,128)(2,1)} %bitcast.29, bf16[128,2048]{1,0:T(8,128)(2,1)} %copy-done.16, bf16[128,2048]{1,0:T(8,128)(2,1)} %copy-done.17, bf16[128,2048]{1,0:T(8,128)(2,1)} %copy-done.18, ...), custom_call_target="tpu_custom_call" | custom-call | tf_op jit(solution)/shard_map/pallas_call | solution.py:54
  65.6 7.1 %collective-permute-done.7.refs_9_ = bf16[2,128,512]{2,1,0:T(8,128)(2,1)S(1)} collective-permute-done((bf16[2,128,512]{2,1,0:T(8,128)(2,1)S(1)}, bf16[2,128,512]{2,1,0:T(8,128)(2,1)S(1)}, u32[]{:S(2)}, u32[]{:S(2)}) %collective-permute-start.7) | collective-permute-done | bytes 262176 | tf_op jit(solution)/shard_map/ppermute | solution.py:23
  72.7 5.6 %collective-permute-done.8.refs_10_ = bf16[2,128,512]{2,1,0:T(8,128)(2,1)S(1)} collective-permute-done((bf16[2,128,512]{2,1,0:T(8,128)(2,1)S(1)}, bf16[2,128,512]{2,1,0:T(8,128)(2,1)S(1)}, u32[]{:S(2)}, u32[]{:S(2)}) %collective-permute-start.8) | collective-permute-done | bytes 262176 | tf_op jit(solution)/shard_map/ppermute | solution.py:23
  78.3 4.3 %collective-permute-done.9.refs_11_ = bf16[2,128,512]{2,1,0:T(8,128)(2,1)S(1)} collective-permute-done((bf16[2,128,512]{2,1,0:T(8,128)(2,1)S(1)}, bf16[2,128,512]{2,1,0:T(8,128)(2,1)S(1)}, u32[]{:S(2)}, u32[]{:S(2)}) %collective-permute-start.9) | collective-permute-done | bytes 262176 | tf_op jit(solution)/shard_map/ppermute | solution.py:23
  83.4 9.6 %shard_map.120 = (f32[512,512]{1,0:T(8,128)}, bf16[512,512]{1,0:T(8,128)(2,1)}, bf16[512,512]{1,0:T(8,128)(2,1)}, bf16[512,512]{1,0:T(8,128)(2,1)}) custom-call(s32[2]{0:T(128)} %pad_add_fusion.place_ref, bf16[1,128,512]{2,1,0:T(8,128)(2,1)} %get-tuple-element.46.refs_0_, bf16[1,128,512]{2,1,0:T(8,128)(2,1)} %copy-done.22, bf16[1,128,512]{2,1,0:T(8,128)(2,1)} %copy-done.23, ...), custom_call_target="tpu_custom_call" | custom-call | tf_op jit(solution)/shard_map/pallas_call | solution.py:54
  94.7 2.5 %collective-permute-start.15 = (bf16[512,512]{1,0:T(8,128)(2,1)}, bf16[512,512]{1,0:T(8,128)(2,1)S(1)}, u32[]{:S(2)}, u32[]{:S(2)}) collective-permute-start(bf16[512,512]{1,0:T(8,128)(2,1)} %get-tuple-element.59), channel_id=1, source_target_pairs={{0,32},{16,48},{32,0},{48,16},{64,96},{80,112},{96,64},{112,80},{1... | collective-permute-start | bytes 1572872 | tf_op jit(solution)/shard_map/ppermute | solution.py:23
  97.2 2.6 %shard_map.121 = (bf16[1,128,512]{2,1,0:T(8,128)(2,1)}, bf16[1,128,512]{2,1,0:T(8,128)(2,1)}, bf16[1,128,512]{2,1,0:T(8,128)(2,1)}, bf16[1,128,512]{2,1,0:T(8,128)(2,1)}) custom-call(s32[2]{0:T(128)} %pad_add_fusion.place_ref, bf16[128,2048]{1,0:T(8,128)(2,1)} %bitcast.35), custom_call_target="tpu_custom_call" | custom-call | tf_op jit(solution)/shard_map/pallas_call | solution.py:54
  101.4 19.8 %collective-permute-done.14 = bf16[1,128,512]{2,1,0:T(8,128)(2,1)S(1)} collective-permute-done((bf16[1,128,512]{2,1,0:T(8,128)(2,1)}, bf16[1,128,512]{2,1,0:T(8,128)(2,1)S(1)}, u32[]{:S(2)}, u32[]{:S(2)}) %collective-permute-start.14) | collective-permute-done | bytes 131104 | tf_op jit(solution)/shard_map/ppermute | solution.py:23
  123.1 6.2 %collective-permute-done.13 = bf16[1,128,512]{2,1,0:T(8,128)(2,1)S(1)} collective-permute-done((bf16[1,128,512]{2,1,0:T(8,128)(2,1)}, bf16[1,128,512]{2,1,0:T(8,128)(2,1)S(1)}, u32[]{:S(2)}, u32[]{:S(2)}) %collective-permute-start.13) | collective-permute-done | bytes 131104 | tf_op jit(solution)/shard_map/ppermute | solution.py:23
  135.4 8.7 %collective-permute-done.28.c1.refs_13_ = bf16[512,512]{1,0:T(8,128)(2,1)S(1)} collective-permute-done((bf16[512,512]{1,0:T(8,128)(2,1)S(1)}, bf16[512,512]{1,0:T(8,128)(2,1)S(1)}, u32[]{:S(2)}, u32[]{:S(2)}) %collective-permute-start.28) | collective-permute-done | bytes 524320 | tf_op jit(solution)/shard_map/ppermute | solution.py:23
  144.1 8.7 %collective-permute-done.29.c2.refs_14_ = bf16[512,512]{1,0:T(8,128)(2,1)S(1)} collective-permute-done((bf16[512,512]{1,0:T(8,128)(2,1)S(1)}, bf16[512,512]{1,0:T(8,128)(2,1)S(1)}, u32[]{:S(2)}, u32[]{:S(2)}) %collective-permute-start.29) | collective-permute-done | bytes 524320 | tf_op jit(solution)/shard_map/ppermute | solution.py:23
  155.1 8.9 %shard_map.126 = (bf16[512,256]{1,0:T(8,128)(2,1)}, bf16[2,512,256]{2,1,0:T(8,128)(2,1)}, bf16[2,512,256]{2,1,0:T(8,128)(2,1)}) custom-call(s32[2]{0:T(128)} %pad_add_fusion.place_ref, bf16[1,128,512]{2,1,0:T(8,128)(2,1)} %get-tuple-element.46.refs_0_, bf16[1,128,512]{2,1,0:T(8,128)(2,1)} %copy-done.22, bf16[1,128,512]{2,1,0:T(8,128)(2,1)} %copy-done.23, ...), custom_call_target="tpu_custom_call" | custom-call | tf_op jit(solution)/shard_map/pallas_call | solution.py:54
  166.9 5.3 %shard_map.122 = (f32[128,2048]{1,0:T(8,128)}, bf16[128,2048]{1,0:T(8,128)(2,1)}, bf16[128,2048]{1,0:T(8,128)(2,1)}, bf16[128,2048]{1,0:T(8,128)(2,1)}) custom-call(s32[2]{0:T(128)} %pad_add_fusion.place_ref, bf16[512,512]{1,0:T(8,128)(2,1)} %copy-done.21, bf16[512,512]{1,0:T(8,128)(2,1)} %copy-done.20, bf16[256,2048]{1,0:T(8,128)(2,1)} %bitcast.26, ...), custom_call_target="tpu_custom_call" | custom-call | tf_op jit(solution)/shard_map/pallas_call | solution.py:54
  173.4 8.9 %shard_map.125 = (bf16[512,256]{1,0:T(8,128)(2,1)}, bf16[2,512,256]{2,1,0:T(8,128)(2,1)}, bf16[2,512,256]{2,1,0:T(8,128)(2,1)}) custom-call(s32[2]{0:T(128)} %pad_add_fusion.place_ref, bf16[1,128,512]{2,1,0:T(8,128)(2,1)} %get-tuple-element.46.refs_0_, bf16[1,128,512]{2,1,0:T(8,128)(2,1)} %copy-done.22, bf16[1,128,512]{2,1,0:T(8,128)(2,1)} %copy-done.23, ...), custom_call_target="tpu_custom_call" | custom-call | tf_op jit(solution)/shard_map/pallas_call | solution.py:54
  186.6 4.9 %shard_map.131 = (f32[256,2048]{1,0:T(8,128)}, bf16[256,2048]{1,0:T(8,128)(2,1)}) custom-call(s32[2]{0:T(128)} %pad_add_fusion.place_ref, bf16[512,512]{1,0:T(8,128)(2,1)} %copy-done.21, bf16[128,2048]{1,0:T(8,128)(2,1)} %bitcast.30, bf16[128,2048]{1,0:T(8,128)(2,1)} %copy-done.16, bf16[128,2048]{1,0:T(8,128)(2,1)} %copy-done.17, bf16[128,2048]{1,0:T(8,128)(2,1)} %copy-done.18), custom_call_target="tpu_custom_call" | custom-call | tf_op jit(solution)/shard_map/pallas_call | solution.py:54
  193.7 3.0 %shard_map.127 = (bf16[4,128,256]{2,1,0:T(8,128)(2,1)}, bf16[4,128,256]{2,1,0:T(8,128)(2,1)}, bf16[4,128,256]{2,1,0:T(8,128)(2,1)}, bf16[4,128,256]{2,1,0:T(8,128)(2,1)}) custom-call(s32[2]{0:T(128)} %pad_add_fusion.place_ref, bf16[2,512,256]{2,1,0:T(8,128)(2,1)} %get-tuple-element.68.a, bf16[2,512,256]{2,1,0:T(8,128)(2,1)} %copy-done.31, ...), custom_call_target="tpu_custom_call" | custom-call | tf_op jit(solution)/shard_map/pallas_call | solution.py:54
  196.8 2.7 %collective-permute-start.33 = (bf16[4,128,256]{2,1,0:T(8,128)(2,1)}, bf16[4,128,256]{2,1,0:T(8,128)(2,1)S(1)}, u32[]{:S(2)}, u32[]{:S(2)}) collective-permute-start(bf16[4,128,256]{2,1,0:T(8,128)(2,1)} %get-tuple-element.74), channel_id=1, source_target_pairs={{0,64},{16,80},{32,96},{48,112},{64,0},{80,16},{96,32},{112,48},{1... | collective-permute-start | bytes 786440 | tf_op jit(solution)/shard_map/ppermute | solution.py:23
  199.5 2.6 %shard_map.124 = bf16[128,2048]{1,0:T(8,128)(2,1)} custom-call(s32[2]{0:T(128)} %pad_add_fusion.place_ref, bf16[512,512]{1,0:T(8,128)(2,1)} %copy-done, bf16[512,512]{1,0:T(8,128)(2,1)} %copy-done.1, bf16[512,512]{1,0:T(8,128)(2,1)} %copy-done.2, bf16[512,512]{1,0:T(8,128)(2,1)} %copy-done.3), custom_call_target="tpu_custom_call" | custom-call | tf_op jit(solution)/shard_map/pallas_call | solution.py:54
  202.1 2.7 %shard_map.129 = (bf16[2,128,256]{2,1,0:T(8,128)(2,1)}, bf16[2,128,256]{2,1,0:T(8,128)(2,1)}, bf16[2,128,256]{2,1,0:T(8,128)(2,1)}, bf16[2,128,256]{2,1,0:T(8,128)(2,1)}) custom-call(s32[2]{0:T(128)} %pad_add_fusion.place_ref, bf16[2,512,256]{2,1,0:T(8,128)(2,1)} %get-tuple-element.76.a, bf16[2,512,256]{2,1,0:T(8,128)(2,1)} %copy-done.32), custom_call_target="tpu_custom_call" | custom-call | tf_op jit(solution)/shard_map/pallas_call | solution.py:54
  206.9 3.7 %collective-permute-done.21 = bf16[128,2048]{1,0:T(8,128)(2,1)S(1)} collective-permute-done((bf16[128,2048]{1,0:T(8,128)(2,1)S(1)}, bf16[128,2048]{1,0:T(8,128)(2,1)S(1)}, u32[]{:S(2)}, u32[]{:S(2)}) %collective-permute-start.21) | collective-permute-done | bytes 524320 | tf_op jit(solution)/shard_map/ppermute | solution.py:23
  210.9 5.3 %collective-permute-done.32.h1.refs_5_ = bf16[4,128,256]{2,1,0:T(8,128)(2,1)S(1)} collective-permute-done((bf16[4,128,256]{2,1,0:T(8,128)(2,1)}, bf16[4,128,256]{2,1,0:T(8,128)(2,1)S(1)}, u32[]{:S(2)}, u32[]{:S(2)}) %collective-permute-start.32) | collective-permute-done | bytes 262176 | tf_op jit(solution)/shard_map/ppermute | solution.py:23
  217.2 3.3 %collective-permute-done.33.h2.refs_6_ = bf16[4,128,256]{2,1,0:T(8,128)(2,1)S(1)} collective-permute-done((bf16[4,128,256]{2,1,0:T(8,128)(2,1)}, bf16[4,128,256]{2,1,0:T(8,128)(2,1)S(1)}, u32[]{:S(2)}, u32[]{:S(2)}) %collective-permute-start.33) | collective-permute-done | bytes 262176 | tf_op jit(solution)/shard_map/ppermute | solution.py:23
  220.4 2.8 %collective-permute-start.38 = (bf16[2,128,256]{2,1,0:T(8,128)(2,1)}, bf16[2,128,256]{2,1,0:T(8,128)(2,1)S(1)}, u32[]{:S(2)}, u32[]{:S(2)}) collective-permute-start(bf16[2,128,256]{2,1,0:T(8,128)(2,1)} %get-tuple-element.81), channel_id=1, source_target_pairs={{0,96},{16,112},{32,64},{48,80},{64,32},{80,48},{96,0},{112,16},{1... | collective-permute-start | bytes 393224 | tf_op jit(solution)/shard_map/ppermute | solution.py:23
  225.0 2.8 %shard_map.128 = bf16[128,2048]{1,0:T(8,128)(2,1)} custom-call(s32[2]{0:T(128)} %pad_add_fusion.place_ref, bf16[4,128,256]{2,1,0:T(8,128)(2,1)} %get-tuple-element.72.h0.refs_4_, bf16[4,128,256]{2,1,0:T(8,128)(2,1)} %copy-done.27, bf16[4,128,256]{2,1,0:T(8,128)(2,1)} %copy-done.28, bf16[4,128,256]{2,1,0:T(8,128)(2,1)} %copy-done.29), custom_call_target="tpu_custom_call" | custom-call | tf_op jit(solution)/shard_map/pallas_call | solution.py:54
  228.6 3.0 %shard_map.130 = (bf16[128,2048]{1,0:T(8,128)(2,1)}, bf16[128,2048]{1,0:T(8,128)(2,1)}) custom-call(s32[2]{0:T(128)} %pad_add_fusion.place_ref, bf16[2,128,256]{2,1,0:T(8,128)(2,1)} %get-tuple-element.78.refs_0_, bf16[2,128,256]{2,1,0:T(8,128)(2,1)} %copy-done.33, bf16[2,128,256]{2,1,0:T(8,128)(2,1)} %copy-done.34, bf16[2,128,256]{2,1,0:T(8,128)(2,1)} %copy-done.35, ...), custom_call_target="tpu_custom_call" | custom-call | tf_op jit(solution)/shard_map/pallas_call | solution.py:54
  (147 shorter events, 56.3 us)
Async XLA Ops:
  1.8 18.9 %collective-permute-start.19 = (bf16[128,2048]{1,0:T(8,128)(2,1)S(1)}, bf16[128,2048]{1,0:T(8,128)(2,1)S(1)}, u32[]{:S(2)}, u32[]{:S(2)}) collective-permute-start(bf16[128,2048]{1,0:T(8,128)(2,1)S(1)} %dynamic-slice_bitcast_fusion), channel_id=1, source_target_pairs={{0,17},{1,16},{2,19},{3,18},{4,21},{5,20},{6,23},{7,22},{8,25},{9,... | collective-permute-start | bytes 1572872 | tf_op jit(solution)/shard_map/ppermute | solution.py:35
  12.4 14.4 %collective-permute-start.10 = (bf16[128,2048]{1,0:T(8,128)(2,1)S(1)}, bf16[128,2048]{1,0:T(8,128)(2,1)S(1)}, u32[]{:S(2)}, u32[]{:S(2)}) collective-permute-start(bf16[128,2048]{1,0:T(8,128)(2,1)S(1)} %dynamic-slice_bitcast_fusion.1), channel_id=1, source_target_pairs={{0,17},{1,16},{2,19},{3,18},{4,21},{5,20},{6,23},{7,22},{8,25},{9,... | collective-permute-start | bytes 1572872 | tf_op jit(solution)/shard_map/ppermute | solution.py:35
  13.0 15.4 %collective-permute-start.24 = (bf16[128,2048]{1,0:T(8,128)(2,1)S(1)}, bf16[128,2048]{1,0:T(8,128)(2,1)S(1)}, u32[]{:S(2)}, u32[]{:S(2)}) collective-permute-start(bf16[128,2048]{1,0:T(8,128)(2,1)S(1)} %bitcast.31), channel_id=1, source_target_pairs={{0,32},{16,48},{32,0},{48,16},{64,96},{80,112},{96,64},{112,80},{1... | collective-permute-start | bytes 1572872 | tf_op jit(solution)/shard_map/ppermute | solution.py:23
  17.5 24.2 %collective-permute-start.25 = (bf16[128,2048]{1,0:T(8,128)(2,1)S(1)}, bf16[128,2048]{1,0:T(8,128)(2,1)S(1)}, u32[]{:S(2)}, u32[]{:S(2)}) collective-permute-start(bf16[128,2048]{1,0:T(8,128)(2,1)S(1)} %bitcast.32), channel_id=1, source_target_pairs={{0,64},{16,80},{32,96},{48,112},{64,0},{80,16},{96,32},{112,48},{1... | collective-permute-start | bytes 1572872 | tf_op jit(solution)/shard_map/ppermute | solution.py:23
  19.1 32.9 %collective-permute-start.26 = (bf16[128,2048]{1,0:T(8,128)(2,1)S(1)}, bf16[128,2048]{1,0:T(8,128)(2,1)S(1)}, u32[]{:S(2)}, u32[]{:S(2)}) collective-permute-start(bf16[128,2048]{1,0:T(8,128)(2,1)S(1)} %bitcast.33), channel_id=1, source_target_pairs={{0,96},{16,112},{32,64},{48,80},{64,32},{80,48},{96,0},{112,16},{1... | collective-permute-start | bytes 1572872 | tf_op jit(solution)/shard_map/ppermute | solution.py:23
  20.7 31.3 %collective-permute-start.20 = (bf16[128,2048]{1,0:T(8,128)(2,1)S(1)}, bf16[128,2048]{1,0:T(8,128)(2,1)S(1)}, u32[]{:S(2)}, u32[]{:S(2)}) collective-permute-start(bf16[128,2048]{1,0:T(8,128)(2,1)S(1)} %collective-permute-done.19.mine), channel_id=1, source_target_pairs={{0,1},{1,0},{2,3},{3,2},{4,5},{5,4},{6,7},{7,6},{8,9},{9,8},{10,11... | collective-permute-start | bytes 1572872 | tf_op jit(solution)/shard_map/ppermute | solution.py:35
  26.8 32.8 %collective-permute-start.3 = (bf16[2,128,512]{2,1,0:T(8,128)(2,1)}, bf16[2,128,512]{2,1,0:T(8,128)(2,1)S(1)}, u32[]{:S(2)}, u32[]{:S(2)}) collective-permute-start(bf16[2,128,512]{2,1,0:T(8,128)(2,1)} %get-tuple-element.51), channel_id=1, source_target_pairs={{0,32},{16,48},{32,0},{48,16},{64,96},{80,112},{96,64},{112,80},{1... | collective-permute-start | bytes 786440 | tf_op jit(solution)/shard_map/ppermute | solution.py:23
  28.4 31.4 %collective-permute-start.4 = (bf16[2,128,512]{2,1,0:T(8,128)(2,1)}, bf16[2,128,512]{2,1,0:T(8,128)(2,1)S(1)}, u32[]{:S(2)}, u32[]{:S(2)}) collective-permute-start(bf16[2,128,512]{2,1,0:T(8,128)(2,1)} %get-tuple-element.52), channel_id=1, source_target_pairs={{0,64},{16,80},{32,96},{48,112},{64,0},{80,16},{96,32},{112,48},{1... | collective-permute-start | bytes 786440 | tf_op jit(solution)/shard_map/ppermute | solution.py:23
  41.7 20.4 %collective-permute-start.5 = (bf16[2,128,512]{2,1,0:T(8,128)(2,1)}, bf16[2,128,512]{2,1,0:T(8,128)(2,1)S(1)}, u32[]{:S(2)}, u32[]{:S(2)}) collective-permute-start(bf16[2,128,512]{2,1,0:T(8,128)(2,1)} %get-tuple-element.53), channel_id=1, source_target_pairs={{0,96},{16,112},{32,64},{48,80},{64,32},{80,48},{96,0},{112,16},{1... | collective-permute-start | bytes 786440 | tf_op jit(solution)/shard_map/ppermute | solution.py:23
  52.0 30.5 %collective-permute-start.11 = (bf16[128,2048]{1,0:T(8,128)(2,1)S(1)}, bf16[128,2048]{1,0:T(8,128)(2,1)S(1)}, u32[]{:S(2)}, u32[]{:S(2)}) collective-permute-start(bf16[128,2048]{1,0:T(8,128)(2,1)S(1)} %collective-permute-done.10.refs_13_.refs_16_), channel_id=1, source_target_pairs={{0,1},{1,0},{2,3},{3,2},{4,5},{5,4},{6,7},{7,6},{8,9},{9,8},{10,11... | collective-permute-start | bytes 1572872 | tf_op jit(solution)/shard_map/ppermute | solution.py:35
  59.7 61.5 %collective-permute-start.27 = (bf16[512,512]{1,0:T(8,128)(2,1)}, bf16[512,512]{1,0:T(8,128)(2,1)S(1)}, u32[]{:S(2)}, u32[]{:S(2)}) collective-permute-start(bf16[512,512]{1,0:T(8,128)(2,1)} %get-tuple-element.67), channel_id=1, source_target_pairs={{0,128},{128,0},{1,129},{129,1},{2,130},{130,2},{3,131},{131,3},{4... | collective-permute-start | bytes 1572872 | tf_op jit(solution)/shard_map/ppermute | solution.py:27
  59.8 12.9 %collective-permute-start.7 = (bf16[2,128,512]{2,1,0:T(8,128)(2,1)S(1)}, bf16[2,128,512]{2,1,0:T(8,128)(2,1)S(1)}, u32[]{:S(2)}, u32[]{:S(2)}) collective-permute-start(bf16[2,128,512]{2,1,0:T(8,128)(2,1)S(1)} %collective-permute-done.3.refs_5_), channel_id=1, source_target_pairs={{0,16},{16,0},{32,48},{48,32},{64,80},{80,64},{96,112},{112,96},{1... | collective-permute-start | bytes 786440 | tf_op jit(solution)/shard_map/ppermute | solution.py:23
  62.1 16.2 %collective-permute-start.8 = (bf16[2,128,512]{2,1,0:T(8,128)(2,1)S(1)}, bf16[2,128,512]{2,1,0:T(8,128)(2,1)S(1)}, u32[]{:S(2)}, u32[]{:S(2)}) collective-permute-start(bf16[2,128,512]{2,1,0:T(8,128)(2,1)S(1)} %collective-permute-done.4.refs_6_), channel_id=1, source_target_pairs={{0,16},{16,0},{32,48},{48,32},{64,80},{80,64},{96,112},{112,96},{1... | collective-permute-start | bytes 786440 | tf_op jit(solution)/shard_map/ppermute | solution.py:23
  63.4 19.2 %collective-permute-start.9 = (bf16[2,128,512]{2,1,0:T(8,128)(2,1)S(1)}, bf16[2,128,512]{2,1,0:T(8,128)(2,1)S(1)}, u32[]{:S(2)}, u32[]{:S(2)}) collective-permute-start(bf16[2,128,512]{2,1,0:T(8,128)(2,1)S(1)} %collective-permute-done.5.refs_7_), channel_id=1, source_target_pairs={{0,16},{16,0},{32,48},{48,32},{64,80},{80,64},{96,112},{112,96},{1... | collective-permute-start | bytes 786440 | tf_op jit(solution)/shard_map/ppermute | solution.py:23
  93.1 38.6 %collective-permute-start.17 = (bf16[512,512]{1,0:T(8,128)(2,1)}, bf16[512,512]{1,0:T(8,128)(2,1)S(1)}, u32[]{:S(2)}, u32[]{:S(2)}) collective-permute-start(bf16[512,512]{1,0:T(8,128)(2,1)} %get-tuple-element.61), channel_id=1, source_target_pairs={{0,96},{16,112},{32,64},{48,80},{64,32},{80,48},{96,0},{112,16},{1... | collective-permute-start | bytes 1572872 | tf_op jit(solution)/shard_map/ppermute | solution.py:23
  94.7 39.3 %collective-permute-start.16 = (bf16[512,512]{1,0:T(8,128)(2,1)}, bf16[512,512]{1,0:T(8,128)(2,1)S(1)}, u32[]{:S(2)}, u32[]{:S(2)}) collective-permute-start(bf16[512,512]{1,0:T(8,128)(2,1)} %get-tuple-element.60), channel_id=1, source_target_pairs={{0,64},{16,80},{32,96},{48,112},{64,0},{80,16},{96,32},{112,48},{1... | collective-permute-start | bytes 1572872 | tf_op jit(solution)/shard_map/ppermute | solution.py:23
  94.7 39.3 %collective-permute-start.15 = (bf16[512,512]{1,0:T(8,128)(2,1)}, bf16[512,512]{1,0:T(8,128)(2,1)S(1)}, u32[]{:S(2)}, u32[]{:S(2)}) collective-permute-start(bf16[512,512]{1,0:T(8,128)(2,1)} %get-tuple-element.59), channel_id=1, source_target_pairs={{0,32},{16,48},{32,0},{48,16},{64,96},{80,112},{96,64},{112,80},{1... | collective-permute-start | bytes 1572872 | tf_op jit(solution)/shard_map/ppermute | solution.py:23
  99.8 21.4 %collective-permute-start.14 = (bf16[1,128,512]{2,1,0:T(8,128)(2,1)}, bf16[1,128,512]{2,1,0:T(8,128)(2,1)S(1)}, u32[]{:S(2)}, u32[]{:S(2)}) collective-permute-start(bf16[1,128,512]{2,1,0:T(8,128)(2,1)} %get-tuple-element.58), channel_id=1, source_target_pairs={{0,96},{16,112},{32,64},{48,80},{64,32},{80,48},{96,0},{112,16},{1... | collective-permute-start | bytes 393224 | tf_op jit(solution)/shard_map/ppermute | solution.py:23
  129.3 14.8 %collective-permute-start.28 = (bf16[512,512]{1,0:T(8,128)(2,1)S(1)}, bf16[512,512]{1,0:T(8,128)(2,1)S(1)}, u32[]{:S(2)}, u32[]{:S(2)}) collective-permute-start(bf16[512,512]{1,0:T(8,128)(2,1)S(1)} %add_convert_fusion.c0.refs_12_), channel_id=1, source_target_pairs={{0,32},{16,48},{32,0},{48,16},{64,96},{80,112},{96,64},{112,80},{1... | collective-permute-start | bytes 1572872 | tf_op jit(solution)/shard_map/ppermute | solution.py:23
  129.3 23.5 %collective-permute-start.29 = (bf16[512,512]{1,0:T(8,128)(2,1)S(1)}, bf16[512,512]{1,0:T(8,128)(2,1)S(1)}, u32[]{:S(2)}, u32[]{:S(2)}) collective-permute-start(bf16[512,512]{1,0:T(8,128)(2,1)S(1)} %add_convert_fusion.c0.refs_12_), channel_id=1, source_target_pairs={{0,64},{16,80},{32,96},{48,112},{64,0},{80,16},{96,32},{112,48},{1... | collective-permute-start | bytes 1572872 | tf_op jit(solution)/shard_map/ppermute | solution.py:23
  131.7 22.5 %collective-permute-start.30 = (bf16[512,512]{1,0:T(8,128)(2,1)S(1)}, bf16[512,512]{1,0:T(8,128)(2,1)S(1)}, u32[]{:S(2)}, u32[]{:S(2)}) collective-permute-start(bf16[512,512]{1,0:T(8,128)(2,1)S(1)} %add_convert_fusion.c0.refs_12_), channel_id=1, source_target_pairs={{0,96},{16,112},{32,64},{48,80},{64,32},{80,48},{96,0},{112,16},{1... | collective-permute-start | bytes 1572872 | tf_op jit(solution)/shard_map/ppermute | solution.py:23
  135.3 30.8 %collective-permute-start.18 = (bf16[512,512]{1,0:T(8,128)(2,1)S(1)}, bf16[512,512]{1,0:T(8,128)(2,1)S(1)}, u32[]{:S(2)}, u32[]{:S(2)}) collective-permute-start(bf16[512,512]{1,0:T(8,128)(2,1)S(1)} %add_convert_fusion.2.own_hid), channel_id=1, source_target_pairs={{0,128},{128,0},{1,129},{129,1},{2,130},{130,2},{3,131},{131,3},{4... | collective-permute-start | bytes 1572872 | tf_op jit(solution)/shard_map/ppermute | solution.py:27
  164.0 27.5 %collective-permute-start.31 = (bf16[2,512,256]{2,1,0:T(8,128)(2,1)}, bf16[2,512,256]{2,1,0:T(8,128)(2,1)S(1)}, u32[]{:S(2)}, u32[]{:S(2)}) collective-permute-start(bf16[2,512,256]{2,1,0:T(8,128)(2,1)} %get-tuple-element.69), channel_id=1, source_target_pairs={{0,16},{16,0},{32,48},{48,32},{64,80},{80,64},{96,112},{112,96},{1... | collective-permute-start | bytes 1572872 | tf_op jit(solution)/shard_map/ppermute | solution.py:23
  172.1 24.6 %collective-permute-start.23 = (bf16[128,2048]{1,0:T(8,128)(2,1)}, bf16[128,2048]{1,0:T(8,128)(2,1)S(1)}, u32[]{:S(2)}, u32[]{:S(2)}) collective-permute-start(bf16[128,2048]{1,0:T(8,128)(2,1)} %get-tuple-element.65), channel_id=1, source_target_pairs={{0,96},{16,112},{32,64},{48,80},{64,32},{80,48},{96,0},{112,16},{1... | collective-permute-start | bytes 1572872 | tf_op jit(solution)/shard_map/ppermute | solution.py:23
  182.3 14.5 %collective-permute-start.35 = (bf16[2,512,256]{2,1,0:T(8,128)(2,1)}, bf16[2,512,256]{2,1,0:T(8,128)(2,1)S(1)}, u32[]{:S(2)}, u32[]{:S(2)}) collective-permute-start(bf16[2,512,256]{2,1,0:T(8,128)(2,1)} %get-tuple-element.77), channel_id=1, source_target_pairs={{0,16},{16,0},{32,48},{48,32},{64,80},{80,64},{96,112},{112,96},{1... | collective-permute-start | bytes 1572872 | tf_op jit(solution)/shard_map/ppermute | solution.py:23
  184.6 20.3 %collective-permute-start.22 = (bf16[128,2048]{1,0:T(8,128)(2,1)S(1)}, bf16[128,2048]{1,0:T(8,128)(2,1)S(1)}, u32[]{:S(2)}, u32[]{:S(2)}) collective-permute-start(bf16[128,2048]{1,0:T(8,128)(2,1)S(1)} %copy-done.37), channel_id=1, source_target_pairs={{0,64},{16,80},{32,96},{48,112},{64,0},{80,16},{96,32},{112,48},{1... | collective-permute-start | bytes 1572872 | tf_op jit(solution)/shard_map/ppermute | solution.py:23
  184.9 25.7 %collective-permute-start.21 = (bf16[128,2048]{1,0:T(8,128)(2,1)S(1)}, bf16[128,2048]{1,0:T(8,128)(2,1)S(1)}, u32[]{:S(2)}, u32[]{:S(2)}) collective-permute-start(bf16[128,2048]{1,0:T(8,128)(2,1)S(1)} %copy-done.36), channel_id=1, source_target_pairs={{0,32},{16,48},{32,0},{48,16},{64,96},{80,112},{96,64},{112,80},{1... | collective-permute-start | bytes 1572872 | tf_op jit(solution)/shard_map/ppermute | solution.py:23
  191.5 40.1 %collective-permute-start.39 = (bf16[256,2048]{1,0:T(8,128)(2,1)}, bf16[256,2048]{1,0:T(8,128)(2,1)S(1)}, u32[]{:S(2)}, u32[]{:S(2)}) collective-permute-start(bf16[256,2048]{1,0:T(8,128)(2,1)} %get-tuple-element.85), channel_id=1, source_target_pairs={{0,16},{16,0},{32,48},{48,32},{64,80},{80,64},{96,112},{112,96},{1... | collective-permute-start | bytes 3145736 | tf_op jit(solution)/shard_map/ppermute | solution.py:23
  196.7 19.5 %collective-permute-start.32 = (bf16[4,128,256]{2,1,0:T(8,128)(2,1)}, bf16[4,128,256]{2,1,0:T(8,128)(2,1)S(1)}, u32[]{:S(2)}, u32[]{:S(2)}) collective-permute-start(bf16[4,128,256]{2,1,0:T(8,128)(2,1)} %get-tuple-element.73), channel_id=1, source_target_pairs={{0,32},{16,48},{32,0},{48,16},{64,96},{80,112},{96,64},{112,80},{1... | collective-permute-start | bytes 786440 | tf_op jit(solution)/shard_map/ppermute | solution.py:23
  196.8 23.6 %collective-permute-start.33 = (bf16[4,128,256]{2,1,0:T(8,128)(2,1)}, bf16[4,128,256]{2,1,0:T(8,128)(2,1)S(1)}, u32[]{:S(2)}, u32[]{:S(2)}) collective-permute-start(bf16[4,128,256]{2,1,0:T(8,128)(2,1)} %get-tuple-element.74), channel_id=1, source_target_pairs={{0,64},{16,80},{32,96},{48,112},{64,0},{80,16},{96,32},{112,48},{1... | collective-permute-start | bytes 786440 | tf_op jit(solution)/shard_map/ppermute | solution.py:23
  204.8 19.5 %collective-permute-start.34 = (bf16[4,128,256]{2,1,0:T(8,128)(2,1)S(1)}, bf16[4,128,256]{2,1,0:T(8,128)(2,1)S(1)}, u32[]{:S(2)}, u32[]{:S(2)}) collective-permute-start(bf16[4,128,256]{2,1,0:T(8,128)(2,1)S(1)} %copy-done.38), channel_id=1, source_target_pairs={{0,96},{16,112},{32,64},{48,80},{64,32},{80,48},{96,0},{112,16},{1... | collective-permute-start | bytes 786440 | tf_op jit(solution)/shard_map/ppermute | solution.py:23
  210.6 17.2 %collective-permute-start.36 = (bf16[2,128,256]{2,1,0:T(8,128)(2,1)}, bf16[2,128,256]{2,1,0:T(8,128)(2,1)S(1)}, u32[]{:S(2)}, u32[]{:S(2)}) collective-permute-start(bf16[2,128,256]{2,1,0:T(8,128)(2,1)} %get-tuple-element.79), channel_id=1, source_target_pairs={{0,32},{16,48},{32,0},{48,16},{64,96},{80,112},{96,64},{112,80},{1... | collective-permute-start | bytes 393224 | tf_op jit(solution)/shard_map/ppermute | solution.py:23
  (47 other events, 668.9 us)
